TPU v7x, 256 devices: a whole 4x4x8 slice. The times are simulated.
256 devices in a mesh: ctx: 64 (over x, z, core), head: 4 (over y).
Axes of the slice: x: 4, y: 4, z: 8, core: 2. Of those that a mesh axis runs over, the one named last changes fastest.
Arguments:
- queries: bfloat16 [16384, 2560], P('ctx', 'head'), may hold values from -130 to 130
- keys: bfloat16 [16384, 2560], P('ctx', 'head'), may hold values from -7 to 7
- values: bfloat16 [16384, 2560], P('ctx', 'head'), may hold values from -6 to 6
- out_weight: bfloat16 [2560, 5120], P('head'), may hold values from -0.125 to 0.125
- reward_grad: bfloat16 [16384, 5120], P('ctx', 'head'), may hold values from -6 to 6
- tile_mask: int32 [128, 10], replicated, may hold values from 0 to 1, as said below
Outputs:
- grad_queries: bfloat16 [16384, 2560], P('ctx', 'head')
- grad_keys: bfloat16 [16384, 2560], P('ctx', 'head')
- grad_values: bfloat16 [16384, 2560], P('ctx', 'head')
Inputs may be any that keep to these rules, and one draw needn't show every extreme that they name: `tile_mask`: entries are 0 or 1. The column 4 + (row % 2), a query tile's own tile, is always 1; columns that name a tile outside the sequence are 0.
All inputs are finite; a program needn't handle non-finite values.
Results may differ from a plain program's by a relative error of at most 0.033.
Values may be sent and summed in bfloat16 or wider, within the bound.
A program may use at most 128 MiB of HBM per device.

v0:
```python
import math

import jax
import jax.numpy as jnp
from jax import lax
from jax.sharding import PartitionSpec as P

HEAD_DIM = 128
TILE = 128
SPAN = 2


def from_behind(array, axis, by):
    length = lax.axis_size(axis)
    pairs = [(i, i + by) for i in range(length) if 0 <= i + by < length]
    return lax.ppermute(array, axis, pairs)


def attend_local(query_blk, key_win, value_win, grad_blk, live_pairs, score_scale):
    scores = (
        jnp.einsum("qhd,khd->hqk", query_blk, key_win, preferred_element_type=jnp.float32)
        * score_scale
    )
    live_three = live_pairs[None, :, :]
    row_max = jnp.max(jnp.where(live_three, scores, -jnp.inf), axis=-1, keepdims=True)
    weights = jnp.where(live_three, jnp.exp(scores - row_max), 0.0)
    totals = jnp.sum(weights, axis=-1, keepdims=True)
    attn_out = (
        jnp.einsum(
            "hqk,khd->hqd",
            weights.astype(jnp.bfloat16),
            value_win,
            preferred_element_type=jnp.float32,
        )
        / totals
    ).astype(jnp.bfloat16)
    grad_heads = jnp.transpose(grad_blk, (1, 0, 2))
    delta = jnp.sum(
        grad_heads.astype(jnp.float32) * attn_out.astype(jnp.float32), axis=-1, keepdims=True
    )
    probs = weights / totals
    grad_value_win = jnp.einsum(
        "hqk,hqd->khd", probs.astype(jnp.bfloat16), grad_heads, preferred_element_type=jnp.float32
    )
    dprobs = jnp.einsum("hqd,khd->hqk", grad_heads, value_win, preferred_element_type=jnp.float32)
    dscores = (probs * (dprobs - delta)).astype(jnp.bfloat16)
    grad_query_blk = (
        jnp.einsum("hqk,khd->qhd", dscores, key_win, preferred_element_type=jnp.float32)
        * score_scale
    ).astype(jnp.bfloat16)
    grad_key_win = (
        jnp.einsum("hqk,qhd->khd", dscores, query_blk, preferred_element_type=jnp.float32)
        * score_scale
    )
    return (grad_query_blk, grad_key_win, grad_value_win)


def local(queries, keys, values, out_weight, reward_grad, tile_mask):
    rows_dev = queries.shape[0]
    feat_width = queries.shape[1]
    head_count = feat_width // HEAD_DIM
    tiles_dev = rows_dev // TILE
    win_tiles = (2 * SPAN + 1) * tiles_dev
    total_tiles = tile_mask.shape[0]
    score_scale = 1.0 / math.sqrt(HEAD_DIM)
    position = lax.axis_index("ctx")
    kv_pair = jnp.stack([keys, values])
    from_below = []
    from_above = []
    for offset in range(1, SPAN + 1):
        from_below.append(from_behind(kv_pair, "ctx", offset))
        from_above.append(from_behind(kv_pair, "ctx", -offset))
    window = jnp.concatenate(from_below[::-1] + [kv_pair] + from_above, axis=1)
    grad_sum = lax.dot_general(
        lax.all_gather(reward_grad, "head", axis=1, tiled=True),
        out_weight,
        (((1,), (1,)), ((), ())),
        preferred_element_type=jnp.float32,
    )
    d_out = grad_sum.astype(jnp.bfloat16)
    mask_rows = lax.dynamic_slice_in_dim(tile_mask, position * tiles_dev, tiles_dev, 0)
    target = (position - SPAN) * tiles_dev + jnp.arange(win_tiles, dtype=jnp.int32)
    tile_live = (mask_rows > 0) & ((target >= 0) & (target < total_tiles))[None, :]
    live_pairs = jnp.broadcast_to(
        tile_live[:, None, :, None], (tiles_dev, TILE, win_tiles, TILE)
    ).reshape(rows_dev, win_tiles * TILE)
    window_len = window.shape[1]
    grad_query_blk, grad_key_win, grad_value_win = attend_local(
        queries.reshape(rows_dev, head_count, HEAD_DIM),
        window[0].reshape(window_len, head_count, HEAD_DIM),
        window[1].reshape(window_len, head_count, HEAD_DIM),
        d_out.reshape(rows_dev, head_count, HEAD_DIM),
        live_pairs,
        score_scale,
    )
    grad_window = jnp.stack(
        [
            grad_key_win.reshape(window_len, feat_width),
            grad_value_win.reshape(window_len, feat_width),
        ]
    ).reshape(2, 2 * SPAN + 1, rows_dev, feat_width)
    slices = [grad_window[:, index] for index in range(2 * SPAN + 1)]
    summed = slices[SPAN]
    for offset in range(1, SPAN + 1):
        summed = summed + from_behind(slices[SPAN - offset], "ctx", -offset)
        summed = summed + from_behind(slices[SPAN + offset], "ctx", offset)
    grad_queries = grad_query_blk.reshape(rows_dev, feat_width)
    return (grad_queries, summed[0].astype(jnp.bfloat16), summed[1].astype(jnp.bfloat16))


def solution(mesh):
    placed = (
        P("ctx", "head"),
        P("ctx", "head"),
        P("ctx", "head"),
        P("head", None),
        P("ctx", "head"),
        P(),
    )
    return jax.shard_map(
        local,
        mesh=mesh,
        in_specs=placed,
        out_specs=(P("ctx", "head"), P("ctx", "head"), P("ctx", "head")),
        check_vma=False,
    )
```

profile of v0, /device:TPU:7, one launch (start us, length us, event | category | flops | bytes accessed | tf_op | source)
XLA Modules:
  0.0 160.9 jit_solution(12788838062469707816)
XLA Ops:
  7.2 0.0 copy-start
  7.2 0.0 copy-start.7
  7.2 0.0 all-gather.2.cloned.1.call-start
  7.2 0.7 all-gather.2.cloned.1.call-update
  7.9 1.1 copy.43
  9.1 1.1 copy.44
  10.2 0.1 pad_maximum_fusion.1
  10.3 3.5 %collective-permute-start = (bf16[2,256,640]{1,2,0:T(8,128)(2,1)S(1)}, bf16[2,256,640]{1,2,0:T(8,128)(2,1)}, u32[]{:S(2)}, u32[]{:S(2)}) collective-permute-start(bf16[2,256,640]{1,2,0:T(8,128)(2,1)S(1)} %pad_maximum_fusion.1), channel_id=1, source_target_pairs={{0,8},{4,12},{8,16},{12,20},{16,24},{20,28},{24,32},{28,36},{32,40... | collective-permute-start | bytes 1966088 | tf_op jit(solution)/shard_map/ppermute | solution.py:16
  13.8 4.4 %collective-permute-start.1 = (bf16[2,256,640]{1,2,0:T(8,128)(2,1)S(1)}, bf16[2,256,640]{1,2,0:T(8,128)(2,1)}, u32[]{:S(2)}, u32[]{:S(2)}) collective-permute-start(bf16[2,256,640]{1,2,0:T(8,128)(2,1)S(1)} %pad_maximum_fusion.1), channel_id=1, source_target_pairs={{0,4},{4,8},{8,12},{12,16},{16,20},{20,24},{24,28},{28,32},{32,36}... | collective-permute-start | bytes 1966088 | tf_op jit(solution)/shard_map/ppermute | solution.py:16
  18.2 3.8 %collective-permute-start.3 = (bf16[2,256,640]{1,2,0:T(8,128)(2,1)S(1)}, bf16[2,256,640]{1,2,0:T(8,128)(2,1)S(1)}, u32[]{:S(2)}, u32[]{:S(2)}) collective-permute-start(bf16[2,256,640]{1,2,0:T(8,128)(2,1)S(1)} %pad_maximum_fusion.1), channel_id=1, source_target_pairs={{8,0},{12,4},{16,8},{20,12},{24,16},{28,20},{32,24},{36,28},{40,32... | collective-permute-start | bytes 1966088 | tf_op jit(solution)/shard_map/ppermute | solution.py:16
  22.1 2.7 %collective-permute-start.2 = (bf16[2,256,640]{1,2,0:T(8,128)(2,1)S(1)}, bf16[2,256,640]{1,2,0:T(8,128)(2,1)}, u32[]{:S(2)}, u32[]{:S(2)}) collective-permute-start(bf16[2,256,640]{1,2,0:T(8,128)(2,1)S(1)} %pad_maximum_fusion.1), channel_id=1, source_target_pairs={{4,0},{8,4},{12,8},{16,12},{20,16},{24,20},{28,24},{32,28},{36,32}... | collective-permute-start | bytes 1966088 | tf_op jit(solution)/shard_map/ppermute | solution.py:16
  24.8 0.0 copy-done
  24.8 0.1 constant_dynamic-slice_fusion
  24.9 0.1 copy.75
  25.0 0.0 copy-done.7
  25.0 0.2 copy.47
  25.2 0.2 broadcast_in_dim.30
  25.4 0.2 copy.82
  25.6 0.5 copy.46
  26.1 6.5 %collective-permute-done = bf16[2,256,640]{1,2,0:T(8,128)(2,1)} collective-permute-done((bf16[2,256,640]{1,2,0:T(8,128)(2,1)S(1)}, bf16[2,256,640]{1,2,0:T(8,128)(2,1)}, u32[]{:S(2)}, u32[]{:S(2)}) %collective-permute-start) | collective-permute-done | bytes 655392 | tf_op jit(solution)/shard_map/ppermute | solution.py:16
  32.6 1.1 constant_dynamic-update-slice_fusion.4
  33.7 1.7 %collective-permute-done.1 = bf16[2,256,640]{1,2,0:T(8,128)(2,1)} collective-permute-done((bf16[2,256,640]{1,2,0:T(8,128)(2,1)S(1)}, bf16[2,256,640]{1,2,0:T(8,128)(2,1)}, u32[]{:S(2)}, u32[]{:S(2)}) %collective-permute-start.1) | collective-permute-done | bytes 655392 | tf_op jit(solution)/shard_map/ppermute | solution.py:16
  35.4 1.1 constant_dynamic-update-slice_fusion.3
  36.6 6.4 %collective-permute-done.2 = bf16[2,256,640]{1,2,0:T(8,128)(2,1)} collective-permute-done((bf16[2,256,640]{1,2,0:T(8,128)(2,1)S(1)}, bf16[2,256,640]{1,2,0:T(8,128)(2,1)}, u32[]{:S(2)}, u32[]{:S(2)}) %collective-permute-start.2) | collective-permute-done | bytes 655392 | tf_op jit(solution)/shard_map/ppermute | solution.py:16
  43.0 1.1 constant_dynamic-update-slice_fusion.1
  44.1 0.0 collective-permute-done.3
  44.2 1.5 fusion.46
  45.6 5.9 %fusion.47 = (f32[5,256]{1,0:T(8,128)S(1)}, f32[5,256,1280]{1,2,0:T(8,128)}) fusion(pred[256,1280]{0,1:T(8,128)(4,1)S(1)} %copy.46, bf16[1280,5,128]{0,2,1:T(8,128)(2,1)S(1)} %bitcast.84, bf16[256,5,128]{0,2,1:T(8,128)(2,1)S(1)} %bitcast.98), kind=kOutput, calls=%fused_computation.65 | convolution fusion | flops 848692480 | bytes 8852480 | tf_op jit(solution)/shard_map/sub | solution.py:26
  51.5 0.0 copy-done.4
  51.5 0.0 all-gather.2.cloned.1.call-done
  51.5 5.9 %convolution_convert_fusion = bf16[256,640]{1,0:T(8,128)(2,1)S(1)} fusion(bf16[256,5120]{1,0:T(8,128)(2,1)} %all-gather.2.cloned.1.call-done, bf16[640,5120]{1,0:T(8,128)(2,1)} %param.9), kind=kOutput, calls=%fused_computation.48 | convolution fusion | flops 1677885440 | bytes 9502720 | tf_op jit(solution)/shard_map/dot_general | solution.py:74
  57.4 0.0 slice-start
  57.5 0.2 copy.50
  57.6 0.0 slice-start.1
  57.6 0.0 copy-start.6
  57.7 6.0 %convolution_bitcast_fusion = f32[1280,5,128]{0,2,1:T(8,128)} fusion(bf16[5,256,128]{1,2,0:T(8,128)(2,1)S(1)} %bitcast.93, f32[5,256,1280]{1,2,0:T(8,128)} %get-tuple-element.21, f32[5,256]{1,0:T(8,128)S(1)} %get-tuple-element.20), kind=kOutput, calls=%fused_computation.18 | convolution fusion | flops 422707200 | bytes 10163200 | tf_op jit(solution)/shard_map/hqk,hqd->khd/dot_general | solution.py:42
  63.7 0.0 slice-done
  63.7 0.0 slice-done.1
  63.7 0.0 copy-done.6
  63.7 0.7 fusion.39
  64.4 1.3 multiply_convert_fusion
  65.8 0.0 copy-start.2
  65.8 1.0 fusion.5
  66.8 0.7 copy-done.2
  67.5 8.3 %copy.57 = f32[1280,5,128]{2,1,0:T(8,128)} copy(f32[1280,5,128]{2,0,1:T(8,128)S(1)} %fusion.5) | data formatting | bytes 6553600 | tf_op jit(solution)/shard_map/mul | solution.py:52
  75.8 3.6 %stack.19 = f32[1,5,256,640]{3,2,1,0:T(8,128)S(1)} reshape(f32[1280,5,128]{2,1,0:T(8,128)} %copy.57) | data formatting | bytes 6553600 | tf_op jit(solution)/shard_map/stack | solution.py:96
  79.4 5.2 %reshape.37 = f32[1,5,256,640]{2,1,3,0:T(8,128)} reshape(f32[1280,5,128]{0,2,1:T(8,128)} %convolution_bitcast_fusion) | data formatting | bytes 6553600 | tf_op jit(solution)/shard_map/stack | solution.py:96
  84.6 5.4 %copy.74 = f32[1,5,256,640]{3,2,1,0:T(8,128)} copy(f32[1,5,256,640]{2,1,3,0:T(8,128)} %reshape.37) | data formatting | bytes 6553600 | tf_op jit(solution)/shard_map/stack | solution.py:96
  90.0 4.3 %fusion.22 = (f32[2,256,640]{2,1,0:T(8,128)}, f32[2,256,640]{2,1,0:T(8,128)}, f32[2,256,640]{2,1,0:T(8,128)}, f32[2,256,640]{2,1,0:T(8,128)}) fusion(f32[1,5,256,640]{3,2,1,0:T(8,128)S(1)} %stack.19, f32[1,5,256,640]{3,2,1,0:T(8,128)} %copy.74), kind=kLoop, calls=%fused_computation.36 | loop fusion | flops 1310720 | bytes 11796480 | tf_op jit(solution)/shard_map/squeeze | solution.py:102
  94.3 3.0 %collective-permute-start.4 = (f32[2,256,640]{2,1,0:T(8,128)}, f32[2,256,640]{2,1,0:T(8,128)}, u32[]{:S(2)}, u32[]{:S(2)}) collective-permute-start(f32[2,256,640]{2,1,0:T(8,128)} %get-tuple-element.12), channel_id=1, source_target_pairs={{4,0},{8,4},{12,8},{16,12},{20,16},{24,20},{28,24},{32,28},{36,32}... | collective-permute-start | bytes 3932168 | tf_op jit(solution)/shard_map/ppermute | solution.py:16
  97.3 2.6 %collective-permute-start.5 = (f32[2,256,640]{2,1,0:T(8,128)}, f32[2,256,640]{2,1,0:T(8,128)}, u32[]{:S(2)}, u32[]{:S(2)}) collective-permute-start(f32[2,256,640]{2,1,0:T(8,128)} %get-tuple-element.13), channel_id=1, source_target_pairs={{0,4},{4,8},{8,12},{12,16},{16,20},{20,24},{24,28},{28,32},{32,36}... | collective-permute-start | bytes 3932168 | tf_op jit(solution)/shard_map/ppermute | solution.py:16
  99.8 3.6 %collective-permute-start.7 = (f32[2,256,640]{2,1,0:T(8,128)}, f32[2,256,640]{2,1,0:T(8,128)}, u32[]{:S(2)}, u32[]{:S(2)}) collective-permute-start(f32[2,256,640]{2,1,0:T(8,128)} %get-tuple-element.14), channel_id=1, source_target_pairs={{0,8},{4,12},{8,16},{12,20},{16,24},{20,28},{24,32},{28,36},{32,40... | collective-permute-start | bytes 3932168 | tf_op jit(solution)/shard_map/ppermute | solution.py:16
  103.4 7.2 %collective-permute-start.6 = (f32[2,256,640]{2,1,0:T(8,128)}, f32[2,256,640]{2,1,0:T(8,128)}, u32[]{:S(2)}, u32[]{:S(2)}) collective-permute-start(f32[2,256,640]{2,1,0:T(8,128)} %get-tuple-element.15), channel_id=1, source_target_pairs={{8,0},{12,4},{16,8},{20,12},{24,16},{28,20},{32,24},{36,28},{40,32... | collective-permute-start | bytes 3932168 | tf_op jit(solution)/shard_map/ppermute | solution.py:16
  110.6 0.0 copy-done.3
  110.6 0.0 copy-done.5
  110.6 1.4 fusion.29
  112.0 1.9 %copy.64 = bf16[256,640]{1,0:T(8,128)(2,1)} copy(bf16[256,640]{0,1:T(8,128)(2,1)} %bitcast.96) | data formatting | bytes 655360
  113.9 4.0 %collective-permute-done.4 = f32[2,256,640]{2,1,0:T(8,128)} collective-permute-done((f32[2,256,640]{2,1,0:T(8,128)}, f32[2,256,640]{2,1,0:T(8,128)}, u32[]{:S(2)}, u32[]{:S(2)}) %collective-permute-start.4) | collective-permute-done | bytes 1310752 | tf_op jit(solution)/shard_map/ppermute | solution.py:16
  117.9 5.2 %collective-permute-done.5 = f32[2,256,640]{2,1,0:T(8,128)} collective-permute-done((f32[2,256,640]{2,1,0:T(8,128)}, f32[2,256,640]{2,1,0:T(8,128)}, u32[]{:S(2)}, u32[]{:S(2)}) %collective-permute-start.5) | collective-permute-done | bytes 1310752 | tf_op jit(solution)/shard_map/ppermute | solution.py:16
  123.1 27.0 %collective-permute-done.7 = f32[2,256,640]{2,1,0:T(8,128)} collective-permute-done((f32[2,256,640]{2,1,0:T(8,128)}, f32[2,256,640]{2,1,0:T(8,128)}, u32[]{:S(2)}, u32[]{:S(2)}) %collective-permute-start.7) | collective-permute-done | bytes 1310752 | tf_op jit(solution)/shard_map/ppermute | solution.py:16
  150.1 0.0 collective-permute-done.6
  150.1 3.0 %fusion.20 = bf16[2,256,640]{2,1,0:T(8,128)(2,1)S(1)} fusion(f32[2,256,640]{2,1,0:T(8,128)} %collective-permute-done.7, f32[2,256,640]{2,1,0:T(8,128)} %collective-permute-done.6, f32[2,256,640]{2,1,0:T(8,128)} %collective-permute-done.5, f32[2,256,640]{2,1,0:T(8,128)} %collective-permute-done.4, f32[1,5,256,640]{3,2,1,0:T(8,128)S(1)} %stack.19, ...), kind=kLoop, calls=%fused_computation.34 | loop fusion | flops 1966080 | bytes 12451840 | tf_op jit(solution)/shard_map/convert.1
  153.2 0.9 slice_bitcast_fusion
  154.1 0.0 copy-done.1
  (9 shorter events, 0.1 us)
Async XLA Ops:
  7.2 17.6 %copy-start = (s32[128,10]{0,1:T(8,128)S(1)}, s32[128,10]{0,1:T(8,128)}, u32[]{:S(2)}) copy-start(s32[128,10]{0,1:T(8,128)} %param.11) | copy-start | bytes 15364
  7.2 17.8 %copy-start.7 = (bf16[256,640]{1,0:T(8,128)(2,1)S(1)}, bf16[256,640]{1,0:T(8,128)(2,1)}, u32[]{:S(2)}) copy-start(bf16[256,640]{1,0:T(8,128)(2,1)} %param.6) | copy-start | bytes 983044
  7.2 44.4 %all-gather.2.cloned.1.call-start = ((), (), s32[]{:S(2)}) async-start(), calls=%async_computation | async-start | bytes 3276800 | tf_op jit(solution)/shard_map/all_gather | solution.py:75
  10.3 22.3 %collective-permute-start = (bf16[2,256,640]{1,2,0:T(8,128)(2,1)S(1)}, bf16[2,256,640]{1,2,0:T(8,128)(2,1)}, u32[]{:S(2)}, u32[]{:S(2)}) collective-permute-start(bf16[2,256,640]{1,2,0:T(8,128)(2,1)S(1)} %pad_maximum_fusion.1), channel_id=1, source_target_pairs={{0,8},{4,12},{8,16},{12,20},{16,24},{20,28},{24,32},{28,36},{32,40... | collective-permute-start | bytes 1966088 | tf_op jit(solution)/shard_map/ppermute | solution.py:16
  13.8 21.6 %collective-permute-start.1 = (bf16[2,256,640]{1,2,0:T(8,128)(2,1)S(1)}, bf16[2,256,640]{1,2,0:T(8,128)(2,1)}, u32[]{:S(2)}, u32[]{:S(2)}) collective-permute-start(bf16[2,256,640]{1,2,0:T(8,128)(2,1)S(1)} %pad_maximum_fusion.1), channel_id=1, source_target_pairs={{0,4},{4,8},{8,12},{12,16},{16,20},{20,24},{24,28},{28,32},{32,36}... | collective-permute-start | bytes 1966088 | tf_op jit(solution)/shard_map/ppermute | solution.py:16
  18.2 25.9 %collective-permute-start.3 = (bf16[2,256,640]{1,2,0:T(8,128)(2,1)S(1)}, bf16[2,256,640]{1,2,0:T(8,128)(2,1)S(1)}, u32[]{:S(2)}, u32[]{:S(2)}) collective-permute-start(bf16[2,256,640]{1,2,0:T(8,128)(2,1)S(1)} %pad_maximum_fusion.1), channel_id=1, source_target_pairs={{8,0},{12,4},{16,8},{20,12},{24,16},{28,20},{32,24},{36,28},{40,32... | collective-permute-start | bytes 1966088 | tf_op jit(solution)/shard_map/ppermute | solution.py:16
  22.1 20.9 %collective-permute-start.2 = (bf16[2,256,640]{1,2,0:T(8,128)(2,1)S(1)}, bf16[2,256,640]{1,2,0:T(8,128)(2,1)}, u32[]{:S(2)}, u32[]{:S(2)}) collective-permute-start(bf16[2,256,640]{1,2,0:T(8,128)(2,1)S(1)} %pad_maximum_fusion.1), channel_id=1, source_target_pairs={{4,0},{8,4},{12,8},{16,12},{20,16},{24,20},{28,24},{32,28},{36,32}... | collective-permute-start | bytes 1966088 | tf_op jit(solution)/shard_map/ppermute | solution.py:16
  45.6 5.9 %copy-start.4 = (bf16[1,1280,640]{1,2,0:T(8,128)(2,1)}, bf16[1,1280,640]{1,2,0:T(8,128)(2,1)S(1)}, u32[]{:S(2)}) copy-start(bf16[1,1280,640]{1,2,0:T(8,128)(2,1)S(1)} %get-tuple-element.17) | copy-start | bytes 4915204
  57.4 6.2 %slice-start = ((s8[6553600]{0:T(1024)(128)(4,1)}), s8[2359296]{0:T(1024)(128)(4,1)S(1)}, s32[]{:S(2)}) async-start(s8[6553600]{0:T(1024)(128)(4,1)} %bitcast.82), calls=%async_computation.1 | async-start | bytes 4718592
  57.6 6.0 %slice-start.1 = ((s8[6553600]{0:T(1024)(128)(4,1)}), s8[4194304]{0:T(1024)(128)(4,1)S(1)}, s32[]{:S(2)}) async-start(s8[6553600]{0:T(1024)(128)(4,1)} %bitcast.82), calls=%async_computation.2 | async-start | bytes 8388608
  57.6 6.0 %copy-start.6 = (bf16[1,1280,640]{1,2,0:T(8,128)(2,1)S(1)}, bf16[1,1280,640]{1,2,0:T(8,128)(2,1)}, u32[]{:S(2)}) copy-start(bf16[1,1280,640]{1,2,0:T(8,128)(2,1)} %get-tuple-element.16) | copy-start | bytes 4915204
  65.8 1.7 %copy-start.2 = (bf16[5,256,1280]{1,2,0:T(8,128)(2,1)}, bf16[5,256,1280]{1,2,0:T(8,128)(2,1)S(1)}, u32[]{:S(2)}) copy-start(bf16[5,256,1280]{1,2,0:T(8,128)(2,1)S(1)} %multiply_convert_fusion) | copy-start | bytes 9830404
  90.0 20.7 %copy-start.3 = (bf16[5,256,1280]{1,2,0:T(8,128)(2,1)S(1)}, bf16[5,256,1280]{1,2,0:T(8,128)(2,1)}, u32[]{:S(2)}) copy-start(bf16[5,256,1280]{1,2,0:T(8,128)(2,1)} %copy-done.2) | copy-start | bytes 9830404
  90.0 20.7 %copy-start.5 = (bf16[1,1280,640]{1,2,0:T(8,128)(2,1)S(1)}, bf16[1,1280,640]{1,2,0:T(8,128)(2,1)}, u32[]{:S(2)}) copy-start(bf16[1,1280,640]{1,2,0:T(8,128)(2,1)} %copy-done.4) | copy-start | bytes 4915204
  94.3 23.6 %collective-permute-start.4 = (f32[2,256,640]{2,1,0:T(8,128)}, f32[2,256,640]{2,1,0:T(8,128)}, u32[]{:S(2)}, u32[]{:S(2)}) collective-permute-start(f32[2,256,640]{2,1,0:T(8,128)} %get-tuple-element.12), channel_id=1, source_target_pairs={{4,0},{8,4},{12,8},{16,12},{20,16},{24,20},{28,24},{32,28},{36,32}... | collective-permute-start | bytes 3932168 | tf_op jit(solution)/shard_map/ppermute | solution.py:16
  97.3 25.8 %collective-permute-start.5 = (f32[2,256,640]{2,1,0:T(8,128)}, f32[2,256,640]{2,1,0:T(8,128)}, u32[]{:S(2)}, u32[]{:S(2)}) collective-permute-start(f32[2,256,640]{2,1,0:T(8,128)} %get-tuple-element.13), channel_id=1, source_target_pairs={{0,4},{4,8},{8,12},{12,16},{16,20},{20,24},{24,28},{28,32},{32,36}... | collective-permute-start | bytes 3932168 | tf_op jit(solution)/shard_map/ppermute | solution.py:16
  99.8 50.3 %collective-permute-start.7 = (f32[2,256,640]{2,1,0:T(8,128)}, f32[2,256,640]{2,1,0:T(8,128)}, u32[]{:S(2)}, u32[]{:S(2)}) collective-permute-start(f32[2,256,640]{2,1,0:T(8,128)} %get-tuple-element.14), channel_id=1, source_target_pairs={{0,8},{4,12},{8,16},{12,20},{16,24},{20,28},{24,32},{28,36},{32,40... | collective-permute-start | bytes 3932168 | tf_op jit(solution)/shard_map/ppermute | solution.py:16
  103.4 46.7 %collective-permute-start.6 = (f32[2,256,640]{2,1,0:T(8,128)}, f32[2,256,640]{2,1,0:T(8,128)}, u32[]{:S(2)}, u32[]{:S(2)}) collective-permute-start(f32[2,256,640]{2,1,0:T(8,128)} %get-tuple-element.15), channel_id=1, source_target_pairs={{8,0},{12,4},{16,8},{20,12},{24,16},{28,20},{32,24},{36,28},{40,32... | collective-permute-start | bytes 3932168 | tf_op jit(solution)/shard_map/ppermute | solution.py:16
  150.1 3.9 %copy-start.1 = (s32[128,10]{0,1:T(8,128)S(1)}, s32[128,10]{0,1:T(8,128)}, u32[]{:S(2)}) copy-start(s32[128,10]{0,1:T(8,128)} %param.11) | copy-start | bytes 15364
Sparse Core Ops, SparseCore 0:
  9.8 40.6 all-gather.1
where the time goes:
time: 162 us; the launch traced here: 161 us
  waiting for transfers between devices  51.5 us (32%)
  local copies, waits for them, and re-layouts  34.6 us (21%)
  starting transfers between devices  30.8 us (19%)
  matrix products  22.3 us (14%)
  between operations  14.3 us (9%)
  other arithmetic  7.47 us (5%)
    ppermute x8, waiting for transfers between devices, from_behind(): return lax.ppermute(array, axis, pairs)  50.8 us
    ppermute x8, starting transfers between devices, from_behind(): return lax.ppermute(array, axis, pairs)  30.8 us
    another operation x3, local copies, waits for them, and re-layouts, local(): jnp.stack([grad_key_win.reshape(window_len, feat_width), grad_value_win.r...  14.1 us
    unnamed x29, local copies, waits for them, and re-layouts  8.71 us
    mul x1, local copies, waits for them, and re-layouts, attend_local(): jnp.einsum('hqk,qhd->khd', dscores, query_blk, preferred_element_type=jnp...  8.34 us
    dot_general x1, matrix products, attend_local(): jnp.einsum('hqk,hqd->khd', probs.astype(jnp.bfloat16), grad_heads, prefer...  6.01 us
    sub x1, matrix products, attend_local(): weights = jnp.where(live_three, jnp.exp(scores - row_max), 0.0)  5.93 us
    dot_general x1, matrix products, local(): lax.dot_general(lax.all_gather(reward_grad, 'head', axis=1, tiled=True),...  5.88 us
  transfers between devices with their start and end apart: 9, of which 6 were waited for; matrix products, arithmetic and copies ran while one was open for 11% of the time, Pallas kernels for 0%

commit v1 on v0

v1 whole, which is shorter than its diff:
```python
import functools
import math

import jax
import jax.numpy as jnp
from jax import lax
from jax.experimental import pallas as pl
from jax.experimental.pallas import tpu as pltpu
from jax.sharding import PartitionSpec as P

HEAD_DIM = 128
TILE = 128
SPAN = 2
SLOTS = 2 * SPAN + 1
OWN = SPAN
ROWS = 2 * TILE
STAT_ROWS = 8
NEG = -1.0e30
LOG2E = 1.4426950408889634
MESH = pl.DeviceIdType.MESH


def dot_nt(a, b):
    return lax.dot_general(a, b, (((1,), (1,)), ((), ())), preferred_element_type=jnp.float32)


def dot_nn(a, b):
    return lax.dot_general(a, b, (((1,), (0,)), ((), ())), preferred_element_type=jnp.float32)


def kernel(
    num_ctx,
    num_head,
    q_hbm,
    k_hbm,
    v_hbm,
    w_hbm,
    g_hbm,
    mask_hbm,
    dq_ref,
    dk_ref,
    dv_ref,
    kwin,
    vwin,
    qwin,
    dwin,
    gwin,
    wv,
    mask_sm,
    acc,
    e_scr,
    pt_scr,
    o_scr,
    linv_scr,
    dcol_scr,
    comb_scr,
    lse_win,
    del_win,
    loc_sem,
    kvq_send,
    kvq_recv,
    y_send,
    y_recv,
    d_send,
    d_recv,
    st_send,
    st_recv,
):
    heads = q_hbm.shape[1] // HEAD_DIM
    feat = g_hbm.shape[1]
    pos = lax.axis_index("ctx")
    hd = lax.axis_index("head")
    par = lax.rem(pos, 2)
    scale = 1.0 / math.sqrt(HEAD_DIM)
    scale2 = scale * LOG2E

    def at_ctx(off):
        return (lax.rem(pos + (off + num_ctx), num_ctx), hd)

    def at_head(off):
        return (pos, lax.rem(hd + (off + num_head), num_head))

    sibling = (pos + 1 - 2 * par, hd)

    local = [
        pltpu.make_async_copy(g_hbm, gwin.at[0], loc_sem.at[0]),
        pltpu.make_async_copy(w_hbm, wv, loc_sem.at[1]),
        pltpu.make_async_copy(q_hbm, qwin.at[OWN], loc_sem.at[2]),
        pltpu.make_async_copy(k_hbm, kwin.at[OWN], loc_sem.at[3]),
        pltpu.make_async_copy(v_hbm, vwin.at[OWN], loc_sem.at[4]),
        pltpu.make_async_copy(mask_hbm, mask_sm, loc_sem.at[5]),
    ]
    for copy in local:
        copy.start()

    barrier = pltpu.get_barrier_semaphore()
    partners = [at_ctx(-2), at_ctx(-1), at_ctx(1), at_ctx(2), at_head(1), at_head(-1)]
    for who in partners:
        pl.semaphore_signal(barrier, inc=1, device_id=who, device_id_type=MESH)
    pl.semaphore_wait(barrier, len(partners))

    def remote(src, dst, ssem, rsem, who):
        return pltpu.make_async_remote_copy(
            src_ref=src, dst_ref=dst, send_sem=ssem, recv_sem=rsem, device_id=who, device_id_type=MESH
        )

    lo, hi = pl.ds(0, TILE), pl.ds(TILE, TILE)
    up, down = at_head(1), at_head(-1)
    y_up_lo = remote(g_hbm.at[lo], gwin.at[1, lo], y_send.at[0], y_recv.at[0], up)
    y_up_hi = remote(g_hbm.at[hi], gwin.at[1, hi], y_send.at[1], y_recv.at[1], up)
    y_dn_hi = remote(g_hbm.at[hi], gwin.at[3, hi], y_send.at[2], y_recv.at[2], down)
    y_dn_lo = remote(g_hbm.at[lo], gwin.at[3, lo], y_send.at[3], y_recv.at[3], down)
    y_fw_lo = remote(gwin.at[1, lo], gwin.at[2, lo], y_send.at[4], y_recv.at[4], up)
    y_fw_hi = remote(gwin.at[3, hi], gwin.at[2, hi], y_send.at[5], y_recv.at[5], down)

    far_slot = 2 * SPAN - 2 * SPAN * par
    relay_dst = 3 - 2 * par
    near_dst = 1 + 2 * par

    def window(src, win, ssem, rsem):
        above = remote(src, win.at[0], ssem.at[0], rsem.at[0], at_ctx(2))
        below = remote(src, win.at[4], ssem.at[1], rsem.at[4], at_ctx(-2))
        near = remote(src, win.at[near_dst], ssem.at[2], rsem.at[near_dst], sibling)
        relay = remote(win.at[far_slot], win.at[relay_dst], ssem.at[3], rsem.at[relay_dst], sibling)
        return above, below, near, relay

    k_above, k_below, k_near, k_relay = window(k_hbm, kwin, kvq_send.at[0], kvq_recv.at[0])
    v_above, v_below, v_near, v_relay = window(v_hbm, vwin, kvq_send.at[1], kvq_recv.at[1])
    q_above, q_below, q_near, q_relay = window(q_hbm, qwin, kvq_send.at[2], kvq_recv.at[2])
    for copy in (y_up_lo, y_dn_hi, k_above, k_below, y_up_hi, y_dn_lo, k_near):
        copy.start()
    for copy in (v_above, v_below, v_near, q_above, q_below, q_near):
        copy.start()

    def got(win, rsem, slot):
        remote(win.at[OWN], win.at[slot], st_send.at[0, 0], rsem.at[slot], sibling).wait_recv()

    def relay_when_far(win, rsem, relay):
        got(win, rsem, 0)
        got(win, rsem, 4)
        relay.start()

    def rest_of(win, rsem):
        got(win, rsem, 1)
        got(win, rsem, 3)

    def features(slot_off):
        src = lax.rem(hd + slot_off, num_head)
        return pl.ds(pl.multiple_of(src * feat, 128), feat)

    local[0].wait()
    local[1].wait()
    acc[...] = dot_nt(gwin[0], wv[:, features(0)])
    for copy in local[2:]:
        copy.wait()

    def live_bias(value):
        return jnp.where(value > 0, 0.0, NEG).astype(jnp.float32)

    q_bias = [[live_bias(mask_sm[2 * pos + r, col]) for col in range(2 * SLOTS)] for r in range(2)]

    relay_when_far(kwin, kvq_recv.at[0], k_relay)
    y_up_lo.wait_recv()
    y_fw_lo.start()
    y_dn_hi.wait_recv()
    y_fw_hi.start()
    rest_of(kwin, kvq_recv.at[0])

    lane = lax.broadcasted_iota(jnp.int32, (ROWS, 128), 1)
    comb_scr[...] = jnp.zeros_like(comb_scr)

    def head_cols(h):
        return pl.ds(pl.multiple_of(h * HEAD_DIM, HEAD_DIM), HEAD_DIM)

    @pl.loop(0, heads)
    def _(h):
        cols = head_cols(h)
        q_h = qwin[OWN, :, cols]
        tops = [None, None]
        for j in range(SLOTS):
            s = dot_nt(q_h, kwin[j, :, cols]) * scale2
            for r in range(2):
                for t in range(2):
                    part = s[r * TILE : (r + 1) * TILE, t * TILE : (t + 1) * TILE] + q_bias[r][2 * j + t]
                    e_scr[h, r * TILE : (r + 1) * TILE, (2 * j + t) * TILE : (2 * j + t + 1) * TILE] = part
                    tops[r] = part if tops[r] is None else jnp.maximum(tops[r], part)
        for r in range(2):
            rows = pl.ds(r * TILE, TILE)
            top = jnp.max(tops[r], axis=1, keepdims=True)
            total = None
            for col in range(2 * SLOTS):
                lanes = pl.ds(col * TILE, TILE)
                e = jnp.exp2(e_scr[h, rows, lanes] - top)
                e_scr[h, rows, lanes] = e
                total = e if total is None else total + e
            total = jnp.sum(total, axis=1, keepdims=True)
            linv_scr[h, rows, :] = jnp.broadcast_to(1.0 / total, (TILE, 128))
            lse = top + jnp.log2(total)
            comb_scr[rows, :] = jnp.where(lane[:TILE] == h, lse, comb_scr[rows, :])

    lse_win[OWN] = jnp.transpose(comb_scr[...])[:STAT_ROWS, :]

    def stats(win, which):
        return [
            remote(
                win.at[OWN],
                win.at[OWN - off],
                st_send.at[which, i],
                st_recv.at[which, OWN - off],
                at_ctx(off),
            )
            for i, off in enumerate((-2, 2, -1, 1))
        ]

    lse_copies = stats(lse_win, 0)
    for copy in lse_copies:
        copy.start()

    relay_when_far(vwin, kvq_recv.at[1], v_relay)
    y_up_hi.wait_recv()
    acc[...] += dot_nt(gwin[1], wv[:, features(num_head - 1)])
    y_dn_lo.wait_recv()
    acc[...] += dot_nt(gwin[3], wv[:, features(1)])
    rest_of(vwin, kvq_recv.at[1])

    @pl.loop(0, heads)
    def _(h):
        cols = head_cols(h)
        out = None
        for j in range(SLOTS):
            e = e_scr[h, :, j * ROWS : (j + 1) * ROWS].astype(jnp.bfloat16)
            part = dot_nn(e, vwin[j, :, cols])
            out = part if out is None else out + part
        o_scr[:, cols] = (out * linv_scr[h]).astype(jnp.bfloat16)

    relay_when_far(qwin, kvq_recv.at[2], q_relay)
    y_fw_lo.wait_recv()
    y_fw_hi.wait_recv()
    d_out = acc[...] + dot_nt(gwin[2], wv[:, features(2)])
    dwin[OWN] = d_out.astype(jnp.bfloat16)

    comb_scr[...] = jnp.zeros_like(comb_scr)

    @pl.loop(0, heads)
    def _(h):
        cols = head_cols(h)
        delta = jnp.sum(
            dwin[OWN, :, cols].astype(jnp.float32) * o_scr[:, cols].astype(jnp.float32), axis=1, keepdims=True
        )
        dcol_scr[h] = jnp.broadcast_to(delta, (ROWS, 128))
        comb_scr[...] = jnp.where(lane == h, delta, comb_scr[...])

    del_win[OWN] = jnp.transpose(comb_scr[...])[:STAT_ROWS, :]

    def d_window(h):
        cols = head_cols(h)
        own = dwin.at[OWN, :, cols]
        above = remote(own, dwin.at[0, :, cols], d_send.at[h, 0], d_recv.at[h, 0], at_ctx(2))
        below = remote(own, dwin.at[4, :, cols], d_send.at[h, 1], d_recv.at[h, 4], at_ctx(-2))
        near = remote(own, dwin.at[near_dst, :, cols], d_send.at[h, 2], d_recv.at[h, near_dst], sibling)
        relay = remote(
            dwin.at[far_slot, :, cols],
            dwin.at[relay_dst, :, cols],
            d_send.at[h, 3],
            d_recv.at[h, relay_dst],
            sibling,
        )
        return above, below, near, relay

    del_copies = stats(del_win, 1)
    for h in range(heads):
        above, below, near, _ = d_window(h)
        above.start()
        below.start()
        near.start()
        if h == 0:
            for copy in del_copies:
                copy.start()

    @pl.loop(0, heads)
    def _(h):
        cols = head_cols(h)
        d_h = dwin[OWN, :, cols]
        delta = dcol_scr[h]
        linv = linv_scr[h]
        out = None
        for j in range(SLOTS):
            dp = dot_nt(d_h, vwin[j, :, cols])
            ds = []
            for t in range(2):
                e = e_scr[h, :, (2 * j + t) * TILE : (2 * j + t + 1) * TILE]
                ds.append((e * linv * (dp[:, t * TILE : (t + 1) * TILE] - delta)).astype(jnp.bfloat16))
            part = dot_nn(jnp.concatenate(ds, axis=1), kwin[j, :, cols])
            out = part if out is None else out + part
        dq_ref[:, cols] = (out * scale).astype(jnp.bfloat16)

    rest_of(qwin, kvq_recv.at[2])
    for slot in (0, 1, 3, 4):
        got(lse_win, st_recv.at[0], slot)

    k_bias = []
    for j in range(SLOTS):
        block = lax.rem(pos + (j - SPAN + num_ctx), num_ctx)
        k_bias.append(
            [[live_bias(mask_sm[2 * block + t, r + 2 * (2 * SPAN - j)]) for r in range(2)] for t in range(2)]
        )

    @pl.loop(0, heads)
    def _(h):
        cols = head_cols(h)
        k_h = kwin[OWN, :, cols]
        for j in range(SLOTS):
            st = dot_nt(k_h, qwin[j, :, cols]) * scale2
            lse = lse_win[j, pl.ds(h, 1), :]
            for t in range(2):
                lse_t = lse[:, t * TILE : (t + 1) * TILE]
                for r in range(2):
                    part = st[r * TILE : (r + 1) * TILE, t * TILE : (t + 1) * TILE]
                    pt_scr[h, j, r * TILE : (r + 1) * TILE, t * TILE : (t + 1) * TILE] = jnp.exp2(
                        part - (lse_t - k_bias[j][t][r])
                    )

    def d_got(h, slot):
        cols = head_cols(h)
        remote(
            dwin.at[OWN, :, cols], dwin.at[slot, :, cols], st_send.at[0, 0], d_recv.at[h, slot], sibling
        ).wait_recv()

    def d_relay(h):
        d_got(h, 0)
        d_got(h, 4)
        d_window(h)[3].start()

    d_relay(0)
    for slot in (0, 1, 3, 4):
        got(del_win, st_recv.at[1], slot)

    @pl.loop(0, heads)
    def _(h):
        @pl.when(h < heads - 1)
        def _():
            d_relay(h + 1)

        d_got(h, 1)
        d_got(h, 3)
        cols = head_cols(h)
        v_h = vwin[OWN, :, cols]
        dk = None
        dv = None
        for j in range(SLOTS):
            d_j = dwin[j, :, cols]
            p = pt_scr[h, j]
            part = dot_nn(p.astype(jnp.bfloat16), d_j)
            dv = part if dv is None else dv + part
            dp = dot_nt(v_h, d_j)
            ds = (p * (dp - del_win[j, pl.ds(h, 1), :])).astype(jnp.bfloat16)
            part = dot_nn(ds, qwin[j, :, cols])
            dk = part if dk is None else dk + part
        dv_ref[:, cols] = dv.astype(jnp.bfloat16)
        dk_ref[:, cols] = (dk * scale).astype(jnp.bfloat16)

    for copy in (y_up_lo, y_up_hi, y_dn_hi, y_dn_lo, y_fw_lo, y_fw_hi):
        copy.wait_send()
    for copies in (
        (k_above, k_below, k_near, k_relay),
        (v_above, v_below, v_near, v_relay),
        (q_above, q_below, q_near, q_relay),
    ):
        for copy in copies:
            copy.wait_send()
    for copy in lse_copies + del_copies:
        copy.wait_send()

    @pl.loop(0, heads)
    def _(h):
        for copy in d_window(h):
            copy.wait_send()


def local(num_ctx, num_head, queries, keys, values, out_weight, reward_grad, tile_mask):
    rows, width = queries.shape
    feat = reward_grad.shape[1]
    heads = width // HEAD_DIM
    out = jax.ShapeDtypeStruct((rows, width), jnp.bfloat16)
    win = pltpu.VMEM((SLOTS, rows, width), jnp.bfloat16)
    stat = pltpu.VMEM((SLOTS, STAT_ROWS, rows), jnp.float32)
    col = pltpu.VMEM((heads, rows, 128), jnp.float32)
    dma = pltpu.SemaphoreType.DMA
    return pl.pallas_call(
        functools.partial(kernel, num_ctx, num_head),
        out_shape=(out, out, out),
        in_specs=[pl.BlockSpec(memory_space=pl.ANY)] * 6,
        out_specs=[pl.BlockSpec(memory_space=pltpu.VMEM)] * 3,
        scratch_shapes=[
            win,
            win,
            win,
            win,
            pltpu.VMEM((num_head, rows, feat), jnp.bfloat16),
            pltpu.VMEM(out_weight.shape, jnp.bfloat16),
            pltpu.SMEM(tile_mask.shape, jnp.int32),
            pltpu.VMEM((rows, width), jnp.float32),
            pltpu.VMEM((heads, rows, SLOTS * rows), jnp.float32),
            pltpu.VMEM((heads, SLOTS, rows, rows), jnp.float32),
            pltpu.VMEM((rows, width), jnp.bfloat16),
            col,
            col,
            pltpu.VMEM((rows, 128), jnp.float32),
            stat,
            stat,
            dma((6,)),
            dma((3, 4)),
            dma((3, SLOTS)),
            dma((6,)),
            dma((6,)),
            dma((heads, 4)),
            dma((heads, SLOTS)),
            dma((2, 4)),
            dma((2, SLOTS)),
        ],
        compiler_params=pltpu.CompilerParams(
            collective_id=0, has_side_effects=True, vmem_limit_bytes=60 * 1024 * 1024
        ),
        name="halo_attention_backward",
    )(queries, keys, values, out_weight, reward_grad, tile_mask)


def solution(mesh):
    placed = (
        P("ctx", "head"),
        P("ctx", "head"),
        P("ctx", "head"),
        P("head", None),
        P("ctx", "head"),
        P(),
    )
    return jax.shard_map(
        functools.partial(local, mesh.shape["ctx"], mesh.shape["head"]),
        mesh=mesh,
        in_specs=placed,
        out_specs=(P("ctx", "head"), P("ctx", "head"), P("ctx", "head")),
        check_vma=False,
    )
```

time: 162 us -> 57.1 us (0.35)
  the two profiles are of different devices: /device:TPU:7 before, /device:TPU:1 now
where the time goes in v1:
time: 57.1 us; the launch traced here: 56.9 us
  Pallas kernels  49.6 us (87%)
  local copies, waits for them, and re-layouts  6.6 us (12%)
  between operations  0.64 us (1%)
    pallas_call x1, Pallas kernels, local(): pl.pallas_call(functools.partial(kernel, num_ctx, num_head), out_shape=(o...  49.6 us
    unnamed x4, local copies, waits for them, and re-layouts  6.6 us

profile of v1, /device:TPU:1, one launch (start us, length us, event | category | flops | bytes accessed | tf_op | source)
XLA Modules:
  0.0 56.9 jit_solution(687951951134945754)
XLA Ops:
  0.6 1.4 %copy.9.mask_hbm = s32[128,10]{1,0:T(8,128)} copy(s32[128,10]{0,1:T(8,128)} %param.11) | data formatting | bytes 10240 | tf_op args[5]
  2.1 49.6 %halo_attention_backward.1 = (bf16[256,640]{1,0:T(8,128)(2,1)}, bf16[256,640]{1,0:T(8,128)(2,1)}, bf16[256,640]{1,0:T(8,128)(2,1)}) custom-call(bf16[256,640]{1,0:T(8,128)(2,1)} %q_hbm.1, bf16[256,640]{1,0:T(8,128)(2,1)} %k_hbm.1, bf16[256,640]{1,0:T(8,128)(2,1)} %v_hbm.1, bf16[640,5120]{1,0:T(8,128)(2,1)} %w_hbm.1, bf16[256,1280]{1,0:T(8,128)(2,1)} %g_hbm.1, ...), custom_call_target="tpu_custom_call" | custom-call | tf_op jit(solution)/shard_map/halo_attention_backward/pallas_call | solution.py:389
  51.7 1.7 %copy.13 = bf16[256,640]{1,0:T(8,128)(2,1)} copy(bf16[256,640]{1,0:T(8,128)(2,1)} %get-tuple-element.6) | data formatting | bytes 655360
  53.4 1.7 %copy.14 = bf16[256,640]{1,0:T(8,128)(2,1)} copy(bf16[256,640]{1,0:T(8,128)(2,1)} %get-tuple-element.7) | data formatting | bytes 655360
  55.1 1.7 %copy.15 = bf16[256,640]{1,0:T(8,128)(2,1)} copy(bf16[256,640]{1,0:T(8,128)(2,1)} %get-tuple-element.8) | data formatting | bytes 655360

commit v2 on v1

v2 whole, which is shorter than its diff:
```python
import functools
import math

import jax
import jax.numpy as jnp
from jax import lax
from jax.experimental import pallas as pl
from jax.experimental.pallas import tpu as pltpu
from jax.sharding import PartitionSpec as P

HEAD_DIM = 128
TILE = 128
SPAN = 2
SLOTS = 2 * SPAN + 1
OWN = SPAN
ROWS = 2 * TILE
STAT_ROWS = 8
NEG = -1.0e30
LOG2E = 1.4426950408889634
VMEM_MB = 60
MESH = pl.DeviceIdType.MESH


def dot_nt(a, b):
    return lax.dot_general(a, b, (((1,), (1,)), ((), ())), preferred_element_type=jnp.float32)


def dot_nn(a, b):
    return lax.dot_general(a, b, (((1,), (0,)), ((), ())), preferred_element_type=jnp.float32)


def kernel(
    num_ctx,
    num_head,
    q_hbm,
    k_hbm,
    v_hbm,
    w_hbm,
    g_hbm,
    mask_hbm,
    dq_ref,
    dk_ref,
    dv_ref,
    kwin,
    vwin,
    qwin,
    dwin,
    gwin,
    wv,
    mask_sm,
    acc,
    e_scr,
    pt_scr,
    o_scr,
    linv_scr,
    dcol_scr,
    dk_acc,
    dv_acc,
    lse_win,
    del_win,
    loc_sem,
    kvq_send,
    kvq_recv,
    y_send,
    y_recv,
    lo_send,
    lo_recv,
    d_send,
    d_recv,
    st_send,
    st_recv,
):
    heads = q_hbm.shape[1] // HEAD_DIM
    feat = g_hbm.shape[1]
    pos = lax.axis_index("ctx")
    hd = lax.axis_index("head")
    par = lax.rem(pos, 2)
    scale = 1.0 / math.sqrt(HEAD_DIM)
    scale2 = scale * LOG2E

    def at_ctx(off):
        return (lax.rem(pos + (off + num_ctx), num_ctx), hd)

    def at_head(off):
        return (pos, lax.rem(hd + (off + num_head), num_head))

    sibling = (pos + 1 - 2 * par, hd)

    local = [
        pltpu.make_async_copy(g_hbm, gwin.at[0], loc_sem.at[0]),
        pltpu.make_async_copy(w_hbm, wv, loc_sem.at[1]),
        pltpu.make_async_copy(q_hbm, qwin.at[OWN], loc_sem.at[2]),
        pltpu.make_async_copy(k_hbm, kwin.at[OWN], loc_sem.at[3]),
        pltpu.make_async_copy(v_hbm, vwin.at[OWN], loc_sem.at[4]),
        pltpu.make_async_copy(mask_hbm, mask_sm, loc_sem.at[5]),
    ]

    barrier = pltpu.get_barrier_semaphore()
    partners = [at_ctx(-2), at_ctx(-1), at_ctx(1), at_ctx(2), at_head(1), at_head(-1)]
    for who in partners:
        pl.semaphore_signal(barrier, inc=1, device_id=who, device_id_type=MESH)
    for copy in local:
        copy.start()
    pl.semaphore_wait(barrier, len(partners))

    def remote(src, dst, ssem, rsem, who):
        return pltpu.make_async_remote_copy(
            src_ref=src, dst_ref=dst, send_sem=ssem, recv_sem=rsem, device_id=who, device_id_type=MESH
        )

    up, down = at_head(1), at_head(-1)

    def quarter(n):
        return pl.ds(n * (ROWS // 4), ROWS // 4)

    y_up = [remote(g_hbm.at[quarter(n)], gwin.at[1, quarter(n)], y_send.at[n], y_recv.at[n], up) for n in range(4)]
    y_dn = [
        remote(g_hbm.at[quarter(n)], gwin.at[3, quarter(n)], y_send.at[4 + n], y_recv.at[4 + n], down)
        for n in range(4)
    ]
    y_fw = [
        remote(
            gwin.at[3 if n % 2 else 1, quarter(n)],
            gwin.at[2, quarter(n)],
            y_send.at[8 + n],
            y_recv.at[8 + n],
            down if n % 2 else up,
        )
        for n in range(4)
    ]

    far_slot = 2 * SPAN - 2 * SPAN * par
    relay_dst = 3 - 2 * par
    near_dst = 1 + 2 * par

    def window(src, win, ssem, rsem, part=None):
        def view(ref):
            return ref if part is None else ref.at[part[0], part[1]]

        return (
            remote(src, view(win.at[0]), ssem.at[0], rsem.at[0], at_ctx(2)),
            remote(src, view(win.at[4]), ssem.at[1], rsem.at[4], at_ctx(-2)),
            remote(src, view(win.at[near_dst]), ssem.at[2], rsem.at[near_dst], sibling),
            remote(
                view(win.at[far_slot]), view(win.at[relay_dst]), ssem.at[3], rsem.at[relay_dst], sibling
            ),
        )

    k_win = window(k_hbm, kwin, kvq_send.at[0], kvq_recv.at[0])
    v_win = window(v_hbm, vwin, kvq_send.at[1], kvq_recv.at[1])
    q_win = window(q_hbm, qwin, kvq_send.at[2], kvq_recv.at[2])
    for copy in (y_up[0], y_dn[1], k_win[0], k_win[1], y_up[1], y_dn[0], k_win[2], y_up[2], y_dn[3]):
        copy.start()
    for copy in v_win[:3] + q_win[:3]:
        copy.start()

    def got(rsem, view, slot):
        remote(view(OWN), view(slot), st_send.at[0, 0], rsem.at[slot], sibling).wait_recv()

    def relay_when_far(rsem, view, relay):
        got(rsem, view, 0)
        got(rsem, view, 4)
        relay.start()

    def rest_of(rsem, view):
        got(rsem, view, 1)
        got(rsem, view, 3)

    def k_view(slot):
        return kwin.at[slot]

    def v_view(slot):
        return vwin.at[slot]

    def q_view(slot):
        return qwin.at[slot]

    def weight(slot):
        src = lax.rem(hd + (num_head - slot), num_head)
        return wv[:, pl.ds(pl.multiple_of(src * feat, 128), feat)]

    def tile_rows(t):
        return slice(t * TILE, (t + 1) * TILE)

    def cols_of(h):
        return slice(h * HEAD_DIM, (h + 1) * HEAD_DIM)

    def whole(win, h):
        return win[:, :, cols_of(h)].reshape(SLOTS * ROWS, HEAD_DIM)

    def half(win, h, t):
        return win[:, tile_rows(t), cols_of(h)].reshape(SLOTS * TILE, HEAD_DIM)

    local[0].wait()
    local[1].wait()
    acc[...] = dot_nt(gwin[0], weight(0))
    for copy in local[2:]:
        copy.wait()

    def live_bias(value):
        return jnp.where(value > 0, 0.0, NEG).astype(jnp.float32)

    q_bias = [[live_bias(mask_sm[col, 2 * pos + r]) for col in range(2 * SLOTS)] for r in range(2)]

    y_up[0].wait_recv()
    y_fw[0].start()
    y_up[3].start()
    y_dn[1].wait_recv()
    y_fw[1].start()
    y_dn[2].start()

    relay_when_far(kvq_recv.at[0], k_view, k_win[3])
    rest_of(kvq_recv.at[0], k_view)

    lane = lax.broadcasted_iota(jnp.int32, (TILE, 128), 1)

    lse_cols = [jnp.zeros((TILE, 128), jnp.float32) for _ in range(2)]
    for h in range(heads):
        q_h = qwin[OWN, :, cols_of(h)]
        s = dot_nt(q_h, whole(kwin, h))
        for r in range(2):
            rows = tile_rows(r)
            top = None
            for col in range(2 * SLOTS):
                lanes = tile_rows(col)
                part = s[rows, lanes] * scale2 + q_bias[r][col]
                e_scr[h, rows, lanes] = part
                top = part if top is None else jnp.maximum(top, part)
            top = jnp.max(top, axis=1, keepdims=True)
            total = None
            for col in range(2 * SLOTS):
                lanes = tile_rows(col)
                e = jnp.exp2(e_scr[h, rows, lanes] - top)
                e_scr[h, rows, lanes] = e
                total = e if total is None else total + e
            total = jnp.sum(total, axis=1, keepdims=True)
            linv_scr[h, rows, :] = jnp.broadcast_to(1.0 / total, (TILE, 128))
            lse_cols[r] = jnp.where(lane == h, top + jnp.log2(total), lse_cols[r])
    for r in range(2):
        lse_win[OWN, :, tile_rows(r)] = jnp.transpose(lse_cols[r])[:STAT_ROWS, :]

    def stats(win, which, t):
        def view(slot):
            return win.at[slot, :, pl.ds(t * TILE, TILE)]

        return [
            remote(view(OWN), view(OWN - off), st_send.at[which, i], st_recv.at[which, OWN - off], at_ctx(off))
            for i, off in enumerate((-2, 2, -1, 1))
        ]

    def stats_got(win, which, t):
        for slot in (0, 1, 3, 4):
            got(st_recv.at[which], lambda s: win.at[s, :, pl.ds(t * TILE, TILE)], slot)

    lse_copies = stats(lse_win, 0, 0) + stats(lse_win, 1, 1)
    for copy in lse_copies:
        copy.start()

    y_up[2].wait_recv()
    y_fw[2].start()
    y_dn[3].wait_recv()
    y_fw[3].start()

    lo, hi = tile_rows(0), tile_rows(1)
    y_up[1].wait_recv()
    y_dn[0].wait_recv()
    acc[lo] += dot_nt(gwin[1, lo], weight(1)) + dot_nt(gwin[3, lo], weight(3))

    relay_when_far(kvq_recv.at[1], v_view, v_win[3])

    y_fw[0].wait_recv()
    y_fw[1].wait_recv()
    dwin[OWN, lo] = (acc[lo] + dot_nt(gwin[2, lo], weight(2))).astype(jnp.bfloat16)
    rest_of(kvq_recv.at[1], v_view)

    for h in range(heads):
        out = dot_nn(e_scr[h].astype(jnp.bfloat16), whole(vwin, h))
        o_scr[:, cols_of(h)] = (out * linv_scr[h]).astype(jnp.bfloat16)

    lo_win = window(dwin.at[OWN, pl.ds(0, TILE)], dwin, lo_send, lo_recv, (pl.ds(0, TILE), slice(None)))
    for copy in lo_win[:3]:
        copy.start()

    def delta_of(t):
        rows = tile_rows(t)
        cols = jnp.zeros((TILE, 128), jnp.float32)
        for h in range(heads):
            delta = jnp.sum(
                dwin[OWN, rows, cols_of(h)].astype(jnp.float32) * o_scr[rows, cols_of(h)].astype(jnp.float32),
                axis=1,
                keepdims=True,
            )
            dcol_scr[h, rows] = jnp.broadcast_to(delta, (TILE, 128))
            cols = jnp.where(lane == h, delta, cols)
        del_win[OWN, :, rows] = jnp.transpose(cols)[:STAT_ROWS, :]

    def own_queries(t):
        rows = tile_rows(t)
        for h in range(heads):
            dp = dot_nt(dwin[OWN, rows, cols_of(h)], whole(vwin, h))
            delta = dcol_scr[h, rows]
            linv = linv_scr[h, rows]
            ds = [
                (e_scr[h, rows, tile_rows(col)] * linv * (dp[:, tile_rows(col)] - delta)).astype(jnp.bfloat16)
                for col in range(2 * SLOTS)
            ]
            out = dot_nn(jnp.concatenate(ds, axis=1), whole(kwin, h))
            dq_ref[rows, cols_of(h)] = (out * scale).astype(jnp.bfloat16)

    delta_of(0)
    del_copies = stats(del_win, 2, 0)
    for copy in del_copies:
        copy.start()
    own_queries(0)

    y_up[3].wait_recv()
    y_dn[2].wait_recv()
    acc[hi] += dot_nt(gwin[1, hi], weight(1)) + dot_nt(gwin[3, hi], weight(3))

    relay_when_far(kvq_recv.at[2], q_view, q_win[3])

    y_fw[2].wait_recv()
    y_fw[3].wait_recv()
    dwin[OWN, hi] = (acc[hi] + dot_nt(gwin[2, hi], weight(2))).astype(jnp.bfloat16)
    delta_of(1)
    hi_copies = stats(del_win, 3, 1)

    def hi_window(h):
        part = (pl.ds(TILE, TILE), pl.ds(h * HEAD_DIM, HEAD_DIM))
        return window(dwin.at[OWN, part[0], part[1]], dwin, d_send.at[h], d_recv.at[h], part)

    hi_win = [hi_window(h) for h in range(heads)]
    for h in range(heads):
        for copy in hi_win[h][:3]:
            copy.start()
        if h == 0:
            for copy in hi_copies:
                copy.start()
    own_queries(1)

    rest_of(kvq_recv.at[2], q_view)
    stats_got(lse_win, 0, 0)
    stats_got(lse_win, 1, 1)

    k_bias = [[None, None], [None, None]]
    for t in range(2):
        for r in range(2):
            pieces = []
            for j in range(SLOTS):
                block = lax.rem(pos + (j - SPAN + num_ctx), num_ctx)
                bias = live_bias(mask_sm[r + 2 * (2 * SPAN - j), 2 * block + t])
                pieces.append(jnp.full((1, TILE), bias, jnp.float32))
            k_bias[t][r] = jnp.concatenate(pieces, axis=1)

    def stat_row(win, h, t):
        return jnp.concatenate([win[j, h : h + 1, tile_rows(t)] for j in range(SLOTS)], axis=1)

    for h in range(heads):
        k_h = kwin[OWN, :, cols_of(h)]
        for t in range(2):
            st = dot_nt(k_h, half(qwin, h, t)) * scale2
            lse = stat_row(lse_win, h, t)
            for r in range(2):
                pt_scr[h, t, tile_rows(r)] = jnp.exp2(st[tile_rows(r)] - (lse - k_bias[t][r]))

    def own_keys(h, t):
        d_t = half(dwin, h, t)
        p = pt_scr[h, t]
        dv = dot_nn(p.astype(jnp.bfloat16), d_t)
        dp = dot_nt(vwin[OWN, :, cols_of(h)], d_t)
        ds = (p * (dp - stat_row(del_win, h, t))).astype(jnp.bfloat16)
        return dot_nn(ds, half(qwin, h, t)), dv

    def lo_view(slot):
        return dwin.at[slot, pl.ds(0, TILE)]

    relay_when_far(lo_recv, lo_view, lo_win[3])
    rest_of(lo_recv, lo_view)
    stats_got(del_win, 2, 0)
    for h in range(heads):
        dk, dv = own_keys(h, 0)
        dk_acc[:, cols_of(h)] = dk
        dv_acc[:, cols_of(h)] = dv

    def hi_view(h):
        return lambda slot: dwin.at[slot, pl.ds(TILE, TILE), pl.ds(h * HEAD_DIM, HEAD_DIM)]

    relay_when_far(d_recv.at[0], hi_view(0), hi_win[0][3])
    stats_got(del_win, 3, 1)
    for h in range(heads):
        if h < heads - 1:
            relay_when_far(d_recv.at[h + 1], hi_view(h + 1), hi_win[h + 1][3])
        rest_of(d_recv.at[h], hi_view(h))
        dk, dv = own_keys(h, 1)
        dv_ref[:, cols_of(h)] = (dv_acc[:, cols_of(h)] + dv).astype(jnp.bfloat16)
        dk_ref[:, cols_of(h)] = ((dk_acc[:, cols_of(h)] + dk) * scale).astype(jnp.bfloat16)

    for copies in [y_up, y_dn, y_fw, k_win, v_win, q_win, lo_win, lse_copies, del_copies, hi_copies] + hi_win:
        for copy in copies:
            copy.wait_send()


def write_out(a_ref, b_ref, c_ref, a_out, b_out, c_out, sems):
    copies = [
        pltpu.make_async_copy(src, dst, sems.at[i])
        for i, (src, dst) in enumerate(((a_ref, a_out), (b_ref, b_out), (c_ref, c_out)))
    ]
    for copy in copies:
        copy.start()
    for copy in copies:
        copy.wait()


def local(num_ctx, num_head, queries, keys, values, out_weight, reward_grad, tile_mask):
    rows, width = queries.shape
    feat = reward_grad.shape[1]
    heads = width // HEAD_DIM
    mask_cols = tile_mask.T
    out = jax.ShapeDtypeStruct((rows, width), jnp.bfloat16)
    win = pltpu.VMEM((SLOTS, rows, width), jnp.bfloat16)
    stat = pltpu.VMEM((SLOTS, STAT_ROWS, rows), jnp.float32)
    col = pltpu.VMEM((heads, rows, 128), jnp.float32)
    full = pltpu.VMEM((rows, width), jnp.float32)
    dma = pltpu.SemaphoreType.DMA
    grads = pl.pallas_call(
        functools.partial(kernel, num_ctx, num_head),
        out_shape=(pltpu.VMEM((rows, width), jnp.bfloat16),) * 3,
        in_specs=[pl.BlockSpec(memory_space=pltpu.HBM)] * 6,
        out_specs=[pl.BlockSpec(memory_space=pltpu.VMEM)] * 3,
        scratch_shapes=[
            win,
            win,
            win,
            win,
            pltpu.VMEM((num_head, rows, feat), jnp.bfloat16),
            pltpu.VMEM(out_weight.shape, jnp.bfloat16),
            pltpu.SMEM(mask_cols.shape, jnp.int32),
            full,
            pltpu.VMEM((heads, rows, SLOTS * rows), jnp.float32),
            pltpu.VMEM((heads, 2, rows, SLOTS * TILE), jnp.float32),
            pltpu.VMEM((rows, width), jnp.bfloat16),
            col,
            col,
            full,
            full,
            stat,
            stat,
            dma((6,)),
            dma((3, 4)),
            dma((3, SLOTS)),
            dma((12,)),
            dma((12,)),
            dma((4,)),
            dma((SLOTS,)),
            dma((heads, 4)),
            dma((heads, SLOTS)),
            dma((4, 4)),
            dma((4, SLOTS)),
        ],
        compiler_params=pltpu.CompilerParams(
            collective_id=0, has_side_effects=True, vmem_limit_bytes=VMEM_MB * 1024 * 1024
        ),
        name="halo_attention_backward",
    )(*[pltpu.with_memory_space_constraint(x, pltpu.HBM) for x in (queries, keys, values, out_weight, reward_grad, mask_cols)])
    return pl.pallas_call(
        write_out,
        out_shape=(out, out, out),
        in_specs=[pl.BlockSpec(memory_space=pltpu.VMEM)] * 3,
        out_specs=[pl.BlockSpec(memory_space=pltpu.HBM)] * 3,
        scratch_shapes=[dma((3,))],
        compiler_params=pltpu.CompilerParams(vmem_limit_bytes=262144),
        name="write_out",
    )(*grads)


def solution(mesh):
    placed = (
        P("ctx", "head"),
        P("ctx", "head"),
        P("ctx", "head"),
        P("head", None),
        P("ctx", "head"),
        P(),
    )
    return jax.shard_map(
        functools.partial(local, mesh.shape["ctx"], mesh.shape["head"]),
        mesh=mesh,
        in_specs=placed,
        out_specs=(P("ctx", "head"), P("ctx", "head"), P("ctx", "head")),
        check_vma=False,
    )
```

time: 57.1 us -> 48.1 us (0.84)
  local copies, waits for them, and re-layouts: 6.6 us -> 0 us
  Pallas kernels: 49.6 us -> 47.3 us
    unnamed x4 -> x0, local copies, waits for them, and re-layouts: 6.6 us -> none
    pallas_call x1 -> x2, Pallas kernels: 49.6 us -> 47.3 us  [the longest x1 46.4 us: local(): pl.pallas_call(functools.partial(kernel, num_ctx, num_head), out_shape=(p...]
where the time goes in v2:
time: 48.1 us; the launch traced here: 48 us
  Pallas kernels  47.3 us (98%)
  between operations  0.64 us (1%)
    pallas_call x1, Pallas kernels, local(): pl.pallas_call(functools.partial(kernel, num_ctx, num_head), out_shape=(p...  46.4 us
    pallas_call x1, Pallas kernels, local(): pl.pallas_call(write_out, out_shape=(out, out, out), in_specs=[pl.BlockSp...  0.97 us

profile of v2, /device:TPU:1, one launch (start us, length us, event | category | flops | bytes accessed | tf_op | source)
XLA Modules:
  0.0 48.0 jit_solution(9759434939676809627)
XLA Ops:
  0.6 46.4 %halo_attention_backward.1 = (bf16[256,640]{1,0:T(8,128)(2,1)S(1)}, bf16[256,640]{1,0:T(8,128)(2,1)S(1)}, bf16[256,640]{1,0:T(8,128)(2,1)S(1)}) custom-call(bf16[256,640]{1,0:T(8,128)(2,1)} %q_hbm.1, bf16[256,640]{1,0:T(8,128)(2,1)} %k_hbm.1, bf16[256,640]{1,0:T(8,128)(2,1)} %v_hbm.1, bf16[640,5120]{1,0:T(8,128)(2,1)} %w_hbm.1, bf16[256,1280]{1,0:T(8,128)(2,1)} %g_hbm.1, ...), custom_call_target="tpu_custom_call" | custom-call | tf_op jit(solution)/shard_map/halo_attention_backward/pallas_call | solution.py:425
  47.0 1.0 %write_out.1 = (bf16[256,640]{1,0:T(8,128)(2,1)}, bf16[256,640]{1,0:T(8,128)(2,1)}, bf16[256,640]{1,0:T(8,128)(2,1)}) custom-call(bf16[256,640]{1,0:T(8,128)(2,1)S(1)} %get-tuple-element.6.a_ref, bf16[256,640]{1,0:T(8,128)(2,1)S(1)} %get-tuple-element.7.b_ref, bf16[256,640]{1,0:T(8,128)(2,1)S(1)} %get-tuple-element.8.c_ref), custom_call_target="tpu_custom_call" | custom-call | tf_op jit(solution)/shard_map/write_out/pallas_call | solution.py:465

commit v3 on v2

--- a/solution.py
+++ b/solution.py
@@ -18,6 +18,7 @@
 NEG = -1.0e30
 LOG2E = 1.4426950408889634
 VMEM_MB = 60
+DIRECT = 1
 MESH = pl.DeviceIdType.MESH
 
 
@@ -86,6 +87,22 @@
 
     sibling = (pos + 1 - 2 * par, hd)
 
+    exists = {
+        off: None if off == 0 else (pos >= -off if off < 0 else pos < num_ctx - off) for off in range(-SPAN, SPAN + 1)
+    }
+    from_relay = jnp.where(par == 0, pos, num_ctx - 1 - pos) > 0
+    relays = jnp.where(par == 0, pos + SPAN, num_ctx + 1 - pos) < num_ctx
+
+    def run(cond, action):
+        if cond is None:
+            action()
+        else:
+            pl.when(cond)(action)
+
+    def start(items):
+        for copy, cond in items:
+            run(cond, copy.start)
+
     local = [
         pltpu.make_async_copy(g_hbm, gwin.at[0], loc_sem.at[0]),
         pltpu.make_async_copy(w_hbm, wv, loc_sem.at[1]),
@@ -96,12 +113,27 @@
     ]
 
     barrier = pltpu.get_barrier_semaphore()
-    partners = [at_ctx(-2), at_ctx(-1), at_ctx(1), at_ctx(2), at_head(1), at_head(-1)]
-    for who in partners:
-        pl.semaphore_signal(barrier, inc=1, device_id=who, device_id_type=MESH)
+
+
+    def greet(who):
+        return lambda: pl.semaphore_signal(barrier, inc=1, device_id=who, device_id_type=MESH)
+
+    arrivals = 2
+    for off in (-2, 2, -1, 1):
+        run(exists[off], greet(at_ctx(off)))
+        arrivals = arrivals + exists[off].astype(jnp.int32)
+    greet(at_head(1))()
+    greet(at_head(-1))()
     for copy in local:
         copy.start()
-    pl.semaphore_wait(barrier, len(partners))
+    for off in (-2, 2, -1, 1):
+
+        @pl.when(jnp.logical_not(exists[off]))
+        def _():
+            for win in (kwin, vwin, qwin, dwin, lse_win, del_win):
+                win[OWN + off] = jnp.zeros(win.shape[1:], win.dtype)
+
+    pl.semaphore_wait(barrier, arrivals)
 
     def remote(src, dst, ssem, rsem, who):
         return pltpu.make_async_remote_copy(
@@ -132,35 +164,47 @@
     far_slot = 2 * SPAN - 2 * SPAN * par
     relay_dst = 3 - 2 * par
     near_dst = 1 + 2 * par
+    early, late = (OWN, 3 - 2 * par), (0, 2 * SPAN, 1 + 2 * par)
 
     def window(src, win, ssem, rsem, part=None):
         def view(ref):
             return ref if part is None else ref.at[part[0], part[1]]
 
+        relay_src, relay_to = view(win.at[far_slot]), view(win.at[relay_dst])
         return (
-            remote(src, view(win.at[0]), ssem.at[0], rsem.at[0], at_ctx(2)),
-            remote(src, view(win.at[4]), ssem.at[1], rsem.at[4], at_ctx(-2)),
-            remote(src, view(win.at[near_dst]), ssem.at[2], rsem.at[near_dst], sibling),
-            remote(
-                view(win.at[far_slot]), view(win.at[relay_dst]), ssem.at[3], rsem.at[relay_dst], sibling
-            ),
+            (remote(src, view(win.at[0]), ssem.at[0], rsem.at[0], at_ctx(2)), exists[2]),
+            (remote(src, view(win.at[4]), ssem.at[1], rsem.at[4], at_ctx(-2)), exists[-2]),
+            (remote(src, view(win.at[near_dst]), ssem.at[2], rsem.at[near_dst], sibling), None),
+            (remote(relay_src, relay_to, ssem.at[3], rsem.at[relay_dst], sibling), relays),
         )
 
     k_win = window(k_hbm, kwin, kvq_send.at[0], kvq_recv.at[0])
     v_win = window(v_hbm, vwin, kvq_send.at[1], kvq_recv.at[1])
-    q_win = window(q_hbm, qwin, kvq_send.at[2], kvq_recv.at[2])
-    for copy in (y_up[0], y_dn[1], k_win[0], k_win[1], y_up[1], y_dn[0], k_win[2], y_up[2], y_dn[3]):
+    q_win = [
+        window(
+            q_hbm.at[pl.ds(t * TILE, TILE)],
+            qwin,
+            kvq_send.at[2 + t],
+            kvq_recv.at[2 + t],
+            (pl.ds(t * TILE, TILE), slice(None)),
+        )
+        for t in range(2)
+    ]
+    y_up[0].start()
+    y_dn[1].start()
+    start(k_win[:2])
+    for copy in (y_up[1], y_dn[0], y_up[2], y_dn[3]):
         copy.start()
-    for copy in v_win[:3] + q_win[:3]:
-        copy.start()
+    start(k_win[2:3] + v_win[:3] + q_win[0][:3] + q_win[1][:3])
 
     def got(rsem, view, slot):
-        remote(view(OWN), view(slot), st_send.at[0, 0], rsem.at[slot], sibling).wait_recv()
+        copy = remote(view(OWN), view(slot), st_send.at[0, 0], rsem.at[slot], sibling)
+        run(exists[slot - OWN], copy.wait_recv)
 
     def relay_when_far(rsem, view, relay):
         got(rsem, view, 0)
         got(rsem, view, 4)
-        relay.start()
+        start([relay])
 
     def rest_of(rsem, view):
         got(rsem, view, 1)
@@ -172,8 +216,8 @@
     def v_view(slot):
         return vwin.at[slot]
 
-    def q_view(slot):
-        return qwin.at[slot]
+    def q_view(t):
+        return lambda slot: qwin.at[slot, pl.ds(t * TILE, TILE)]
 
     def weight(slot):
         src = lax.rem(hd + (num_head - slot), num_head)
@@ -188,8 +232,8 @@
     def whole(win, h):
         return win[:, :, cols_of(h)].reshape(SLOTS * ROWS, HEAD_DIM)
 
-    def half(win, h, t):
-        return win[:, tile_rows(t), cols_of(h)].reshape(SLOTS * TILE, HEAD_DIM)
+    def half(win, h, t, slots):
+        return jnp.concatenate([win[j, tile_rows(t), cols_of(h)] for j in slots], axis=0)
 
     local[0].wait()
     local[1].wait()
@@ -197,10 +241,13 @@
     for copy in local[2:]:
         copy.wait()
 
-    def live_bias(value):
-        return jnp.where(value > 0, 0.0, NEG).astype(jnp.float32)
-
-    q_bias = [[live_bias(mask_sm[col, 2 * pos + r]) for col in range(2 * SLOTS)] for r in range(2)]
+    def live_bias(value, off):
+        live = value > 0 if exists[off] is None else jnp.logical_and(value > 0, exists[off])
+        return jnp.where(live, 0.0, NEG).astype(jnp.float32)
+
+    q_bias = [
+        [live_bias(mask_sm[col, 2 * pos + r], col // 2 - SPAN) for col in range(2 * SLOTS)] for r in range(2)
+    ]
 
     y_up[0].wait_recv()
     y_fw[0].start()
@@ -244,17 +291,15 @@
             return win.at[slot, :, pl.ds(t * TILE, TILE)]
 
         return [
-            remote(view(OWN), view(OWN - off), st_send.at[which, i], st_recv.at[which, OWN - off], at_ctx(off))
+            (
+                remote(view(OWN), view(OWN - off), st_send.at[which, i], st_recv.at[which, OWN - off], at_ctx(off)),
+                exists[off],
+            )
             for i, off in enumerate((-2, 2, -1, 1))
         ]
 
-    def stats_got(win, which, t):
-        for slot in (0, 1, 3, 4):
-            got(st_recv.at[which], lambda s: win.at[s, :, pl.ds(t * TILE, TILE)], slot)
-
     lse_copies = stats(lse_win, 0, 0) + stats(lse_win, 1, 1)
-    for copy in lse_copies:
-        copy.start()
+    start(lse_copies)
 
     y_up[2].wait_recv()
     y_fw[2].start()
@@ -278,8 +323,7 @@
         o_scr[:, cols_of(h)] = (out * linv_scr[h]).astype(jnp.bfloat16)
 
     lo_win = window(dwin.at[OWN, pl.ds(0, TILE)], dwin, lo_send, lo_recv, (pl.ds(0, TILE), slice(None)))
-    for copy in lo_win[:3]:
-        copy.start()
+    start(lo_win[:3])
 
     def delta_of(t):
         rows = tile_rows(t)
@@ -307,17 +351,92 @@
             out = dot_nn(jnp.concatenate(ds, axis=1), whole(kwin, h))
             dq_ref[rows, cols_of(h)] = (out * scale).astype(jnp.bfloat16)
 
+    def slot_bias(j, t, r):
+        block = lax.rem(pos + (j - SPAN + num_ctx), num_ctx)
+        there = jnp.logical_and(pos + j >= SPAN, pos + j < num_ctx + SPAN)
+        live = jnp.logical_and(mask_sm[r + 2 * (2 * SPAN - j), 2 * block + t] > 0, there)
+        return jnp.full((1, TILE), jnp.where(live, 0.0, NEG), jnp.float32)
+
+    def stat_row(win, h, t, slots):
+        return jnp.concatenate([win[j, h : h + 1, tile_rows(t)] for j in slots], axis=1)
+
+    def lanes_of(slots):
+        return slice(0, 2 * TILE) if slots is early else slice(2 * TILE, SLOTS * TILE)
+
+    def weights_t(t, slots):
+        bias = [jnp.concatenate([slot_bias(j, t, r) for j in slots], axis=1) for r in range(2)]
+        for h in range(heads):
+            st = dot_nt(kwin[OWN, :, cols_of(h)], half(qwin, h, t, slots)) * scale2
+            lse = stat_row(lse_win, h, t, slots)
+            for r in range(2):
+                pt_scr[h, t, tile_rows(r), lanes_of(slots)] = jnp.exp2(st[tile_rows(r)] - (lse - bias[r]))
+
+    def own_keys(h, t, slots):
+        d_t = half(dwin, h, t, slots)
+        p = pt_scr[h, t, :, lanes_of(slots)]
+        dv = dot_nn(p.astype(jnp.bfloat16), d_t)
+        dp = dot_nt(vwin[OWN, :, cols_of(h)], d_t)
+        ds = (p * (dp - stat_row(del_win, h, t, slots))).astype(jnp.bfloat16)
+        return dot_nn(ds, half(qwin, h, t, slots)), dv
+
+    def add_keys(h, t, slots, first=False):
+        dk, dv = own_keys(h, t, slots)
+        if first:
+            dk_acc[:, cols_of(h)] = dk
+            dv_acc[:, cols_of(h)] = dv
+        else:
+            dk_acc[:, cols_of(h)] += dk
+            dv_acc[:, cols_of(h)] += dv
+
+    def got_at(rsem, win, t, slot, cols=slice(None)):
+        rows = pl.ds(t * TILE, TILE)
+        remote(win.at[OWN, rows, cols], win.at[slot, rows, cols], st_send.at[0, 0], rsem.at[slot], sibling).wait_recv()
+
+    def near_stats(win, which, t):
+        lanes = pl.ds(t * TILE, TILE)
+        remote(
+            win.at[OWN, :, lanes],
+            win.at[early[1], :, lanes],
+            st_send.at[0, 0],
+            st_recv.at[which, early[1]],
+            sibling,
+        ).wait_recv()
+
+    def far_stats(win, which, t):
+        view = lambda slot: win.at[slot, :, pl.ds(t * TILE, TILE)]
+        got(st_recv.at[which], view, 0)
+        got(st_recv.at[which], view, 4)
+        relayed(st_recv.at[which], view)
+
+    def relayed(rsem, view):
+        copy = remote(view(OWN), view(late[2]), st_send.at[0, 0], rsem.at[late[2]], sibling)
+        run(from_relay, copy.wait_recv)
+
     delta_of(0)
     del_copies = stats(del_win, 2, 0)
-    for copy in del_copies:
-        copy.start()
+    start(del_copies)
     own_queries(0)
 
+    got_at(kvq_recv.at[2], qwin, 0, early[1])
+    got_at(kvq_recv.at[3], qwin, 1, early[1])
+    near_stats(lse_win, 0, 0)
+    near_stats(lse_win, 1, 1)
+    weights_t(0, early)
+    weights_t(1, early)
+    relay_when_far(kvq_recv.at[2], q_view(0), q_win[0][3])
     y_up[3].wait_recv()
     y_dn[2].wait_recv()
     acc[hi] += dot_nt(gwin[1, hi], weight(1)) + dot_nt(gwin[3, hi], weight(3))
-
-    relay_when_far(kvq_recv.at[2], q_view, q_win[3])
+    got_at(lo_recv, dwin, 0, early[1])
+    near_stats(del_win, 2, 0)
+    for h in range(heads):
+        add_keys(h, 0, early, first=True)
+
+    relayed(kvq_recv.at[2], q_view(0))
+    far_stats(lse_win, 0, 0)
+    far_stats(lse_win, 1, 1)
+    weights_t(0, late)
+    relay_when_far(kvq_recv.at[3], q_view(1), q_win[1][3])
 
     y_fw[2].wait_recv()
     y_fw[3].wait_recv()
@@ -325,79 +444,74 @@
     delta_of(1)
     hi_copies = stats(del_win, 3, 1)
 
-    def hi_window(h):
-        part = (pl.ds(TILE, TILE), pl.ds(h * HEAD_DIM, HEAD_DIM))
-        return window(dwin.at[OWN, part[0], part[1]], dwin, d_send.at[h], d_recv.at[h], part)
-
-    hi_win = [hi_window(h) for h in range(heads)]
-    for h in range(heads):
-        for copy in hi_win[h][:3]:
-            copy.start()
-        if h == 0:
-            for copy in hi_copies:
-                copy.start()
+    def hi_part(h):
+        return pl.ds(TILE, TILE), pl.ds(h * HEAD_DIM, HEAD_DIM)
+
+    def hi_view(h):
+        return lambda slot: dwin.at[slot, hi_part(h)[0], hi_part(h)[1]]
+
+    hi_win = [window(hi_view(h)(OWN), dwin, d_send.at[h], d_recv.at[h], hi_part(h)) for h in range(heads)]
+    for h in range(heads - DIRECT, heads):
+        view = hi_view(h)
+        straight = remote(
+            view(OWN),
+            view(relay_dst),
+            d_send.at[h, 3],
+            d_recv.at[h, relay_dst],
+            (lax.rem(pos + (2 * par - 1 + num_ctx), num_ctx), hd),
+        )
+        hi_win[h] = hi_win[h][:3] + ((straight, from_relay),)
+    start(hi_win[0][:3] + tuple(hi_copies))
+    for h in range(1, heads):
+        start(hi_win[h] if h >= heads - DIRECT else hi_win[h][:3])
+
+    def hi_relay(h):
+        if h < heads - DIRECT:
+            relay_when_far(d_recv.at[h], hi_view(h), hi_win[h][3])
+
+    relayed(kvq_recv.at[3], q_view(1))
+    weights_t(1, late)
     own_queries(1)
-
-    rest_of(kvq_recv.at[2], q_view)
-    stats_got(lse_win, 0, 0)
-    stats_got(lse_win, 1, 1)
-
-    k_bias = [[None, None], [None, None]]
-    for t in range(2):
-        for r in range(2):
-            pieces = []
-            for j in range(SLOTS):
-                block = lax.rem(pos + (j - SPAN + num_ctx), num_ctx)
-                bias = live_bias(mask_sm[r + 2 * (2 * SPAN - j), 2 * block + t])
-                pieces.append(jnp.full((1, TILE), bias, jnp.float32))
-            k_bias[t][r] = jnp.concatenate(pieces, axis=1)
-
-    def stat_row(win, h, t):
-        return jnp.concatenate([win[j, h : h + 1, tile_rows(t)] for j in range(SLOTS)], axis=1)
-
-    for h in range(heads):
-        k_h = kwin[OWN, :, cols_of(h)]
-        for t in range(2):
-            st = dot_nt(k_h, half(qwin, h, t)) * scale2
-            lse = stat_row(lse_win, h, t)
-            for r in range(2):
-                pt_scr[h, t, tile_rows(r)] = jnp.exp2(st[tile_rows(r)] - (lse - k_bias[t][r]))
-
-    def own_keys(h, t):
-        d_t = half(dwin, h, t)
-        p = pt_scr[h, t]
-        dv = dot_nn(p.astype(jnp.bfloat16), d_t)
-        dp = dot_nt(vwin[OWN, :, cols_of(h)], d_t)
-        ds = (p * (dp - stat_row(del_win, h, t))).astype(jnp.bfloat16)
-        return dot_nn(ds, half(qwin, h, t)), dv
 
     def lo_view(slot):
         return dwin.at[slot, pl.ds(0, TILE)]
 
     relay_when_far(lo_recv, lo_view, lo_win[3])
-    rest_of(lo_recv, lo_view)
-    stats_got(del_win, 2, 0)
+    near_stats(del_win, 3, 1)
     for h in range(heads):
-        dk, dv = own_keys(h, 0)
-        dk_acc[:, cols_of(h)] = dk
-        dv_acc[:, cols_of(h)] = dv
-
-    def hi_view(h):
-        return lambda slot: dwin.at[slot, pl.ds(TILE, TILE), pl.ds(h * HEAD_DIM, HEAD_DIM)]
-
-    relay_when_far(d_recv.at[0], hi_view(0), hi_win[0][3])
-    stats_got(del_win, 3, 1)
-    for h in range(heads):
-        if h < heads - 1:
-            relay_when_far(d_recv.at[h + 1], hi_view(h + 1), hi_win[h + 1][3])
-        rest_of(d_recv.at[h], hi_view(h))
-        dk, dv = own_keys(h, 1)
+        got_at(d_recv.at[h], dwin, 1, early[1], hi_part(h)[1])
+        add_keys(h, 1, early)
+    hi_relay(0)
+    relayed(lo_recv, lo_view)
+    far_stats(del_win, 2, 0)
+    add_keys(0, 0, late)
+    add_keys(1, 0, late)
+    hi_relay(1)
+    add_keys(2, 0, late)
+    add_keys(3, 0, late)
+    hi_relay(2)
+    add_keys(4, 0, late)
+    far_stats(del_win, 3, 1)
+
+    def finish(h):
+        if h >= heads - DIRECT:
+            got(d_recv.at[h], hi_view(h), 0)
+            got(d_recv.at[h], hi_view(h), 4)
+        relayed(d_recv.at[h], hi_view(h))
+        dk, dv = own_keys(h, 1, late)
         dv_ref[:, cols_of(h)] = (dv_acc[:, cols_of(h)] + dv).astype(jnp.bfloat16)
         dk_ref[:, cols_of(h)] = ((dk_acc[:, cols_of(h)] + dk) * scale).astype(jnp.bfloat16)
 
-    for copies in [y_up, y_dn, y_fw, k_win, v_win, q_win, lo_win, lse_copies, del_copies, hi_copies] + hi_win:
-        for copy in copies:
-            copy.wait_send()
+    for h in range(heads):
+        if h + 3 < heads:
+            hi_relay(h + 3)
+        finish(h)
+
+    for copy in y_up + y_dn + y_fw:
+        copy.wait_send()
+    for items in [k_win, v_win, *q_win, lo_win, lse_copies, del_copies, hi_copies, *hi_win]:
+        for copy, cond in items:
+            run(cond, copy.wait_send)
 
 
 def write_out(a_ref, b_ref, c_ref, a_out, b_out, c_out, sems):
@@ -446,8 +560,8 @@
             stat,
             stat,
             dma((6,)),
-            dma((3, 4)),
-            dma((3, SLOTS)),
+            dma((4, 4)),
+            dma((4, SLOTS)),
             dma((12,)),
             dma((12,)),
             dma((4,)),

time: 48.1 us -> 44.8 us (0.931)
  the two profiles are of different devices: /device:TPU:1 before, /device:TPU:7 now
where the time goes in v3:
time: 44.8 us
  Pallas kernels  44 us (98%)
  between operations  0.8 us (2%)
    pallas_call x1, Pallas kernels, local(): pl.pallas_call(functools.partial(kernel, num_ctx, num_head), out_shape=(p...  43 us
    pallas_call x1, Pallas kernels, local(): pl.pallas_call(write_out, out_shape=(out, out, out), in_specs=[pl.BlockSp...  0.97 us

profile of v3, /device:TPU:7, one launch (start us, length us, event | category | flops | bytes accessed | tf_op | source)
XLA Modules:
  0.0 44.8 jit_solution(10556146261977050287)
XLA Ops:
  0.6 43.0 %halo_attention_backward.1 = (bf16[256,640]{1,0:T(8,128)(2,1)S(1)}, bf16[256,640]{1,0:T(8,128)(2,1)S(1)}, bf16[256,640]{1,0:T(8,128)(2,1)S(1)}) custom-call(bf16[256,640]{1,0:T(8,128)(2,1)} %q_hbm.1, bf16[256,640]{1,0:T(8,128)(2,1)} %k_hbm.1, bf16[256,640]{1,0:T(8,128)(2,1)} %v_hbm.1, bf16[640,5120]{1,0:T(8,128)(2,1)} %w_hbm.1, bf16[256,1280]{1,0:T(8,128)(2,1)} %g_hbm.1, ...), custom_call_target="tpu_custom_call" | custom-call | tf_op jit(solution)/shard_map/halo_attention_backward/pallas_call | solution.py:539
  43.6 1.0 %write_out.1 = (bf16[256,640]{1,0:T(8,128)(2,1)}, bf16[256,640]{1,0:T(8,128)(2,1)}, bf16[256,640]{1,0:T(8,128)(2,1)}) custom-call(bf16[256,640]{1,0:T(8,128)(2,1)S(1)} %get-tuple-element.6.a_ref, bf16[256,640]{1,0:T(8,128)(2,1)S(1)} %get-tuple-element.7.b_ref, bf16[256,640]{1,0:T(8,128)(2,1)S(1)} %get-tuple-element.8.c_ref), custom_call_target="tpu_custom_call" | custom-call | tf_op jit(solution)/shard_map/write_out/pallas_call | solution.py:579

commit v4 on v3

--- a/solution.py
+++ b/solution.py
@@ -18,7 +18,7 @@
 NEG = -1.0e30
 LOG2E = 1.4426950408889634
 VMEM_MB = 60
-DIRECT = 1
+GROUPS = ((0, 3), (3, 5))
 MESH = pl.DeviceIdType.MESH
 
 
@@ -163,6 +163,9 @@
 
     far_slot = 2 * SPAN - 2 * SPAN * par
     relay_dst = 3 - 2 * par
+    ahead = 4 * par - 2
+    relays_back = jnp.logical_and(pos - ahead >= 0, pos - ahead < num_ctx)
+    relays_on = jnp.logical_and(pos + ahead >= 0, pos + ahead < num_ctx)
     near_dst = 1 + 2 * par
     early, late = (OWN, 3 - 2 * par), (0, 2 * SPAN, 1 + 2 * par)
 
@@ -172,8 +175,8 @@
 
         relay_src, relay_to = view(win.at[far_slot]), view(win.at[relay_dst])
         return (
-            (remote(src, view(win.at[0]), ssem.at[0], rsem.at[0], at_ctx(2)), exists[2]),
-            (remote(src, view(win.at[4]), ssem.at[1], rsem.at[4], at_ctx(-2)), exists[-2]),
+            (remote(src, view(win.at[4 * (1 - par)]), ssem.at[0], rsem.at[4 * (1 - par)], at_ctx(ahead)), relays_on),
+            (remote(src, view(win.at[4 * par]), ssem.at[1], rsem.at[4 * par], at_ctx(-ahead)), relays_back),
             (remote(src, view(win.at[near_dst]), ssem.at[2], rsem.at[near_dst], sibling), None),
             (remote(relay_src, relay_to, ssem.at[3], rsem.at[relay_dst], sibling), relays),
         )
@@ -202,11 +205,20 @@
         run(exists[slot - OWN], copy.wait_recv)
 
     def relay_when_far(rsem, view, relay):
-        got(rsem, view, 0)
-        got(rsem, view, 4)
-        start([relay])
+        copy = remote(view(OWN), view(far_slot), st_send.at[0, 0], rsem.at[far_slot], sibling)
+
+        @pl.when(relays)
+        def _():
+            copy.wait_recv()
+            relay[0].start()
+
+    def other_far(rsem, view):
+        slot = 2 * SPAN - far_slot
+        copy = remote(view(OWN), view(slot), st_send.at[0, 0], rsem.at[slot], sibling)
+        run(from_relay, copy.wait_recv)
 
     def rest_of(rsem, view):
+        other_far(rsem, view)
         got(rsem, view, 1)
         got(rsem, view, 3)
 
@@ -404,11 +416,13 @@
 
     def far_stats(win, which, t):
         view = lambda slot: win.at[slot, :, pl.ds(t * TILE, TILE)]
-        got(st_recv.at[which], view, 0)
-        got(st_recv.at[which], view, 4)
-        relayed(st_recv.at[which], view)
+        for slot in (0, 4):
+            got(st_recv.at[which], view, slot)
+        copy = remote(view(OWN), view(late[2]), st_send.at[0, 0], st_recv.at[which, late[2]], sibling)
+        run(from_relay, copy.wait_recv)
 
     def relayed(rsem, view):
+        other_far(rsem, view)
         copy = remote(view(OWN), view(late[2]), st_send.at[0, 0], rsem.at[late[2]], sibling)
         run(from_relay, copy.wait_recv)
 
@@ -444,30 +458,24 @@
     delta_of(1)
     hi_copies = stats(del_win, 3, 1)
 
-    def hi_part(h):
-        return pl.ds(TILE, TILE), pl.ds(h * HEAD_DIM, HEAD_DIM)
-
-    def hi_view(h):
-        return lambda slot: dwin.at[slot, hi_part(h)[0], hi_part(h)[1]]
-
-    hi_win = [window(hi_view(h)(OWN), dwin, d_send.at[h], d_recv.at[h], hi_part(h)) for h in range(heads)]
-    for h in range(heads - DIRECT, heads):
-        view = hi_view(h)
-        straight = remote(
-            view(OWN),
-            view(relay_dst),
-            d_send.at[h, 3],
-            d_recv.at[h, relay_dst],
-            (lax.rem(pos + (2 * par - 1 + num_ctx), num_ctx), hd),
-        )
-        hi_win[h] = hi_win[h][:3] + ((straight, from_relay),)
+    groups = GROUPS
+
+    def hi_part(g):
+        first, last = groups[g]
+        return pl.ds(TILE, TILE), pl.ds(first * HEAD_DIM, (last - first) * HEAD_DIM)
+
+    def hi_view(g):
+        return lambda slot: dwin.at[slot, hi_part(g)[0], hi_part(g)[1]]
+
+    hi_win = [
+        window(hi_view(g)(OWN), dwin, d_send.at[g], d_recv.at[g], hi_part(g)) for g in range(len(groups))
+    ]
     start(hi_win[0][:3] + tuple(hi_copies))
-    for h in range(1, heads):
-        start(hi_win[h] if h >= heads - DIRECT else hi_win[h][:3])
-
-    def hi_relay(h):
-        if h < heads - DIRECT:
-            relay_when_far(d_recv.at[h], hi_view(h), hi_win[h][3])
+    for items in hi_win[1:]:
+        start(items[:3])
+
+    def hi_relay(g):
+        relay_when_far(d_recv.at[g], hi_view(g), hi_win[g][3])
 
     relayed(kvq_recv.at[3], q_view(1))
     weights_t(1, late)
@@ -478,34 +486,29 @@
 
     relay_when_far(lo_recv, lo_view, lo_win[3])
     near_stats(del_win, 3, 1)
-    for h in range(heads):
-        got_at(d_recv.at[h], dwin, 1, early[1], hi_part(h)[1])
-        add_keys(h, 1, early)
-    hi_relay(0)
+    for g, (first, last) in enumerate(groups):
+        got_at(d_recv.at[g], dwin, 1, early[1], hi_part(g)[1])
+        for h in range(first, last):
+            add_keys(h, 1, early)
     relayed(lo_recv, lo_view)
     far_stats(del_win, 2, 0)
-    add_keys(0, 0, late)
-    add_keys(1, 0, late)
-    hi_relay(1)
-    add_keys(2, 0, late)
-    add_keys(3, 0, late)
-    hi_relay(2)
-    add_keys(4, 0, late)
+    for h in range(heads):
+        add_keys(h, 0, late)
+        if h == 2:
+            hi_relay(0)
     far_stats(del_win, 3, 1)
 
     def finish(h):
-        if h >= heads - DIRECT:
-            got(d_recv.at[h], hi_view(h), 0)
-            got(d_recv.at[h], hi_view(h), 4)
-        relayed(d_recv.at[h], hi_view(h))
         dk, dv = own_keys(h, 1, late)
         dv_ref[:, cols_of(h)] = (dv_acc[:, cols_of(h)] + dv).astype(jnp.bfloat16)
         dk_ref[:, cols_of(h)] = ((dk_acc[:, cols_of(h)] + dk) * scale).astype(jnp.bfloat16)
 
-    for h in range(heads):
-        if h + 3 < heads:
-            hi_relay(h + 3)
-        finish(h)
+    for g, (first, last) in enumerate(groups):
+        if g == 0:
+            hi_relay(1)
+        relayed(d_recv.at[g], hi_view(g))
+        for h in range(first, last):
+            finish(h)
 
     for copy in y_up + y_dn + y_fw:
         copy.wait_send()

time: 44.8 us -> 44.1 us (0.984)
  Pallas kernels: 44 us -> 43.2 us
    pallas_call x1, Pallas kernels: 43 us -> 42.2 us  [local(): pl.pallas_call(functools.partial(kernel, num_ctx, num_head), out_shape=(p...]
where the time goes in v4:
time: 44.1 us; the launch traced here: 44 us
  Pallas kernels  43.2 us (98%)
  between operations  0.8 us (2%)
    pallas_call x1, Pallas kernels, local(): pl.pallas_call(functools.partial(kernel, num_ctx, num_head), out_shape=(p...  42.2 us
    pallas_call x1, Pallas kernels, local(): pl.pallas_call(write_out, out_shape=(out, out, out), in_specs=[pl.BlockSp...  0.97 us

profile of v4, /device:TPU:7, one launch (start us, length us, event | category | flops | bytes accessed | tf_op | source)
XLA Modules:
  0.0 44.0 jit_solution(15714511021073435262)
XLA Ops:
  0.6 42.2 %halo_attention_backward.1 = (bf16[256,640]{1,0:T(8,128)(2,1)S(1)}, bf16[256,640]{1,0:T(8,128)(2,1)S(1)}, bf16[256,640]{1,0:T(8,128)(2,1)S(1)}) custom-call(bf16[256,640]{1,0:T(8,128)(2,1)} %q_hbm.1, bf16[256,640]{1,0:T(8,128)(2,1)} %k_hbm.1, bf16[256,640]{1,0:T(8,128)(2,1)} %v_hbm.1, bf16[640,5120]{1,0:T(8,128)(2,1)} %w_hbm.1, bf16[256,1280]{1,0:T(8,128)(2,1)} %g_hbm.1, ...), custom_call_target="tpu_custom_call" | custom-call | tf_op jit(solution)/shard_map/halo_attention_backward/pallas_call | solution.py:542
  42.9 1.0 %write_out.1 = (bf16[256,640]{1,0:T(8,128)(2,1)}, bf16[256,640]{1,0:T(8,128)(2,1)}, bf16[256,640]{1,0:T(8,128)(2,1)}) custom-call(bf16[256,640]{1,0:T(8,128)(2,1)S(1)} %get-tuple-element.6.a_ref, bf16[256,640]{1,0:T(8,128)(2,1)S(1)} %get-tuple-element.7.b_ref, bf16[256,640]{1,0:T(8,128)(2,1)S(1)} %get-tuple-element.8.c_ref), custom_call_target="tpu_custom_call" | custom-call | tf_op jit(solution)/shard_map/write_out/pallas_call | solution.py:582

commit v5 on v4

--- a/solution.py
+++ b/solution.py
@@ -504,11 +504,11 @@
         dk_ref[:, cols_of(h)] = ((dk_acc[:, cols_of(h)] + dk) * scale).astype(jnp.bfloat16)
 
     for g, (first, last) in enumerate(groups):
-        if g == 0:
-            hi_relay(1)
         relayed(d_recv.at[g], hi_view(g))
         for h in range(first, last):
             finish(h)
+            if h == 0:
+                hi_relay(1)
 
     for copy in y_up + y_dn + y_fw:
         copy.wait_send()

time: 44.1 us -> 44.8 us (1.016)
  Pallas kernels: 43.2 us -> 43.9 us
    pallas_call x1, Pallas kernels: 42.2 us -> 42.9 us  [local(): pl.pallas_call(functools.partial(kernel, num_ctx, num_head), out_shape=(p...]
where the time goes in v5:
time: 44.8 us; the launch traced here: 44.7 us
  Pallas kernels  43.9 us (98%)
  between operations  0.8 us (2%)
    pallas_call x1, Pallas kernels, local(): pl.pallas_call(functools.partial(kernel, num_ctx, num_head), out_shape=(p...  42.9 us
    pallas_call x1, Pallas kernels, local(): pl.pallas_call(write_out, out_shape=(out, out, out), in_specs=[pl.BlockSp...  0.97 us

profile of v5, /device:TPU:7, one launch (start us, length us, event | category | flops | bytes accessed | tf_op | source)
XLA Modules:
  0.0 44.7 jit_solution(17184160264744191834)
XLA Ops:
  0.6 42.9 %halo_attention_backward.1 = (bf16[256,640]{1,0:T(8,128)(2,1)S(1)}, bf16[256,640]{1,0:T(8,128)(2,1)S(1)}, bf16[256,640]{1,0:T(8,128)(2,1)S(1)}) custom-call(bf16[256,640]{1,0:T(8,128)(2,1)} %q_hbm.1, bf16[256,640]{1,0:T(8,128)(2,1)} %k_hbm.1, bf16[256,640]{1,0:T(8,128)(2,1)} %v_hbm.1, bf16[640,5120]{1,0:T(8,128)(2,1)} %w_hbm.1, bf16[256,1280]{1,0:T(8,128)(2,1)} %g_hbm.1, ...), custom_call_target="tpu_custom_call" | custom-call | tf_op jit(solution)/shard_map/halo_attention_backward/pallas_call | solution.py:542
  43.5 1.0 %write_out.1 = (bf16[256,640]{1,0:T(8,128)(2,1)}, bf16[256,640]{1,0:T(8,128)(2,1)}, bf16[256,640]{1,0:T(8,128)(2,1)}) custom-call(bf16[256,640]{1,0:T(8,128)(2,1)S(1)} %get-tuple-element.6.a_ref, bf16[256,640]{1,0:T(8,128)(2,1)S(1)} %get-tuple-element.7.b_ref, bf16[256,640]{1,0:T(8,128)(2,1)S(1)} %get-tuple-element.8.c_ref), custom_call_target="tpu_custom_call" | custom-call | tf_op jit(solution)/shard_map/write_out/pallas_call | solution.py:582
